TPU v7x, 32 devices: a whole 2x2x4 slice. The times are simulated.
32 devices in a mesh: dp: 8 (over z, y), tensor: 4 (over x, core).
Axes of the slice: x: 2, y: 2, z: 4, core: 2. Of those that a mesh axis runs over, the one named last changes fastest.
Arguments:
- layer_input: bfloat16 [16, 1024, 768], P('dp', 'tensor'), may hold values from -6 to 6
- cotangent: bfloat16 [16, 1024, 768], P('dp', 'tensor'), may hold values from -6 to 6
- segment_ids: int32 [16, 1024], P('dp'), may hold values from 0 to 15, never falling along the last dimension, each value on 1 to 512 neighbouring positions
- query_weight: bfloat16 [768, 768], P('dp', 'tensor'), may hold values from -0.21875 to 0.21875
- key_weight: bfloat16 [768, 768], P('dp', 'tensor'), may hold values from -0.21875 to 0.21875
- value_weight: bfloat16 [768, 768], P('dp', 'tensor'), may hold values from -0.21875 to 0.21875
- output_weight: bfloat16 [768, 768], P('tensor', 'dp'), may hold values from -0.875 to 0.875
- gate_weight: bfloat16 [768, 3072], P('dp', 'tensor'), may hold values from -0.21875 to 0.21875
- up_weight: bfloat16 [768, 3072], P('dp', 'tensor'), may hold values from -0.21875 to 0.21875
- down_weight: bfloat16 [3072, 768], P('tensor', 'dp'), may hold values from -0.109375 to 0.109375
- first_gain: float32 [768], replicated, may hold values from 0.5 to 1.5
- first_bias: float32 [768], replicated, may hold values from -1 to 1
- second_gain: float32 [768], replicated, may hold values from 0.5 to 1.5
- second_bias: float32 [768], replicated, may hold values from -1 to 1
Outputs:
- output: bfloat16 [16, 1024, 768], P('dp', 'tensor')
- grad_input: bfloat16 [16, 1024, 768], P('dp', 'tensor')
- grad_query_weight: float32 [768, 768], P('dp', 'tensor')
- grad_key_weight: float32 [768, 768], P('dp', 'tensor')
- grad_value_weight: float32 [768, 768], P('dp', 'tensor')
- grad_output_weight: float32 [768, 768], P('tensor', 'dp')
- grad_gate_weight: float32 [768, 3072], P('dp', 'tensor')
- grad_up_weight: float32 [768, 3072], P('dp', 'tensor')
- grad_down_weight: float32 [3072, 768], P('tensor', 'dp')
- grad_first_gain: float32 [768], replicated
- grad_first_bias: float32 [768], replicated
- grad_second_gain: float32 [768], replicated
- grad_second_bias: float32 [768], replicated
Inputs may be any that keep to these rules, and one draw needn't show every extreme that they name: `segment_ids`: ids never fall along a packed row and attention only joins tokens of equal id within one row; a document has 1 to 512 tokens, and some document has exactly that many.
All inputs are finite; a program needn't handle non-finite values.
Results may differ from a plain program's by a relative error of at most 0.023.
Values may be sent and summed in bfloat16 or wider, within the bound.
A program may use at most 128 MiB of HBM per device.

v0:
```python
import jax
import jax.numpy as jnp
from jax import lax
from jax.sharding import PartitionSpec as P

HD = 64


eps_norm = 1e-06
rope_base = 1000.0
mask_fill = -1e30


def layer_norm(field_rows, gain_vec, bias_vec):
    row_mean = jnp.mean(field_rows, axis=-1, keepdims=True)
    centred = field_rows - row_mean
    variance = jnp.mean(centred * centred, axis=-1, keepdims=True)
    return centred * lax.rsqrt(variance + eps_norm) * gain_vec + bias_vec


def rotary_tables(length, head_dim):
    half_dim = head_dim // 2
    frequency = rope_base ** (-(2.0 * jnp.arange(half_dim, dtype=jnp.float32)) / head_dim)
    angles = jnp.arange(length, dtype=jnp.float32)[:, None] * frequency[None, :]
    return (jnp.cos(angles), jnp.sin(angles))


def rotate(heads_data, cos_table, sine_table):
    half_dim = heads_data.shape[-1] // 2
    first_half = heads_data[..., :half_dim]
    second_half = heads_data[..., half_dim:]
    cos_part = cos_table[:, None, :]
    sine_part = sine_table[:, None, :]
    return jnp.concatenate(
        [
            first_half * cos_part - second_half * sine_part,
            second_half * cos_part + first_half * sine_part,
        ],
        axis=-1,
    )


def swiglu(gate_pre, up_pre):
    return jax.nn.silu(gate_pre) * up_pre


def contract_rows(left, right):
    return lax.dot_general(
        left, right, (((0,), (0,)), ((), ())), preferred_element_type=jnp.float32
    )


def times_transpose(left, right):
    return lax.dot_general(
        left, right, (((1,), (1,)), ((), ())), preferred_element_type=jnp.float32
    )


def per_device(
    layer_input,
    cotangent,
    segment_ids,
    query_weight,
    key_weight,
    value_weight,
    output_weight,
    gate_weight,
    up_weight,
    down_weight,
    first_gain,
    first_bias,
    second_gain,
    second_bias,
):
    model_width = layer_input.shape[2]
    length = segment_ids.shape[1]
    block_rows = min(512, length)
    block_count = length // block_rows
    local_heads = query_weight.shape[1] // HD
    local_width = local_heads * HD
    score_scale = HD ** (-0.5)
    cos_table, sine_table = rotary_tables(length, HD)

    def fetch_weights():
        row_parts = (
            lax.all_gather(query_weight, "dp", axis=0, tiled=True),
            lax.all_gather(key_weight, "dp", axis=0, tiled=True),
            lax.all_gather(value_weight, "dp", axis=0, tiled=True),
            lax.all_gather(gate_weight, "dp", axis=0, tiled=True),
            lax.all_gather(up_weight, "dp", axis=0, tiled=True),
        )
        col_parts = (
            lax.all_gather(output_weight, "dp", axis=1, tiled=True),
            lax.all_gather(down_weight, "dp", axis=1, tiled=True),
        )
        return tuple(row_parts) + tuple(col_parts)

    def micro_step(weights, row_input, row_cotangent, segment_row):
        query_full, key_full, value_full, gate_full, up_full, output_full, down_full = weights
        full_input = lax.all_gather(row_input, "tensor", axis=0, tiled=True)
        query_pre = jnp.dot(full_input, query_full, preferred_element_type=jnp.float32).reshape(
            length, local_heads, HD
        )
        key_pre = jnp.dot(full_input, key_full, preferred_element_type=jnp.float32).reshape(
            length, local_heads, HD
        )
        value_rows = (
            jnp.dot(full_input, value_full, preferred_element_type=jnp.float32)
            .astype(jnp.bfloat16)
            .reshape(length, local_heads, HD)
        )
        query_rows = rotate(query_pre, cos_table, sine_table).astype(jnp.bfloat16)
        key_rows = rotate(key_pre, cos_table, sine_table).astype(jnp.bfloat16)
        query_blocks = query_rows.reshape(block_count, block_rows, local_heads, HD)
        segment_blocks = segment_row.reshape(block_count, block_rows)

        def block_scores(query_block, segment_block):
            scores = (
                jnp.einsum(
                    "qhd,khd->hqk", query_block, key_rows, preferred_element_type=jnp.float32
                )
                * score_scale
            )
            allowed = segment_block[:, None] == segment_row[None, :]
            return jnp.where(allowed[None, :, :], scores, mask_fill)

        def attend_forward(block_inputs):
            scores = block_scores(block_inputs[0], block_inputs[1])
            row_max = jnp.max(scores, axis=-1, keepdims=True)
            exponent_terms = jnp.exp(scores - row_max)
            row_total = jnp.sum(exponent_terms, axis=-1, keepdims=True)
            probabilities = (exponent_terms / row_total).astype(jnp.bfloat16)
            mixed_rows = jnp.einsum(
                "hqk,khd->qhd", probabilities, value_rows, preferred_element_type=jnp.float32
            )
            return (mixed_rows, (row_max + jnp.log(row_total))[..., 0])

        mixed_blocks, log_totals = lax.map(attend_forward, (query_blocks, segment_blocks))
        attended = mixed_blocks.reshape(length, local_width).astype(jnp.bfloat16)
        attention_branch = lax.psum_scatter(
            jnp.dot(attended, output_full, preferred_element_type=jnp.float32).astype(jnp.bfloat16),
            "tensor",
            scatter_dimension=0,
            tiled=True,
        ).astype(jnp.float32)
        first_sum = row_input.astype(jnp.float32) + attention_branch
        hidden_state, first_back = jax.vjp(layer_norm, first_sum, first_gain, first_bias)
        full_hidden = lax.all_gather(
            hidden_state.astype(jnp.bfloat16), "tensor", axis=0, tiled=True
        )
        gate_pre = jnp.dot(full_hidden, gate_full, preferred_element_type=jnp.float32)
        up_pre = jnp.dot(full_hidden, up_full, preferred_element_type=jnp.float32)
        activated_exact, swiglu_back = jax.vjp(swiglu, gate_pre, up_pre)
        activated = activated_exact.astype(jnp.bfloat16)
        feed_branch = lax.psum_scatter(
            jnp.dot(activated, down_full, preferred_element_type=jnp.float32).astype(jnp.bfloat16),
            "tensor",
            scatter_dimension=0,
            tiled=True,
        ).astype(jnp.float32)
        layer_output, second_back = jax.vjp(
            layer_norm, hidden_state + feed_branch, second_gain, second_bias
        )
        grad_second_sum, grad_second_gain, grad_second_bias = second_back(
            row_cotangent.astype(jnp.float32)
        )
        grad_second_full = lax.all_gather(
            grad_second_sum.astype(jnp.bfloat16), "tensor", axis=0, tiled=True
        )
        grad_activated = times_transpose(grad_second_full, down_full)
        grad_down = contract_rows(activated, grad_second_full)
        grad_gate_pre, grad_up_pre = swiglu_back(grad_activated)
        gate_low = grad_gate_pre.astype(jnp.bfloat16)
        up_low = grad_up_pre.astype(jnp.bfloat16)
        grad_hidden = grad_second_sum + lax.psum_scatter(
            (times_transpose(gate_low, gate_full) + times_transpose(up_low, up_full)).astype(
                jnp.bfloat16
            ),
            "tensor",
            scatter_dimension=0,
            tiled=True,
        ).astype(jnp.float32)
        grad_gate = contract_rows(full_hidden, gate_low)
        grad_up = contract_rows(full_hidden, up_low)
        grad_first_sum, grad_first_gain, grad_first_bias = first_back(grad_hidden)
        grad_first_full = lax.all_gather(
            grad_first_sum.astype(jnp.bfloat16), "tensor", axis=0, tiled=True
        )
        grad_attended = (
            times_transpose(grad_first_full, output_full)
            .astype(jnp.bfloat16)
            .reshape(block_count, block_rows, local_heads, HD)
        )
        grad_output = contract_rows(attended, grad_first_full)

        def attend_backward(sums_carry, block_inputs):
            key_sum, value_sum = sums_carry
            query_block, segment_block, log_block, grad_block = block_inputs
            scores = block_scores(query_block, segment_block)
            probabilities = jnp.exp(scores - log_block[..., None])
            grad_softmax = jnp.einsum(
                "qhd,khd->hqk", grad_block, value_rows, preferred_element_type=jnp.float32
            )
            value_sum = value_sum + jnp.einsum(
                "hqk,qhd->khd",
                probabilities.astype(jnp.bfloat16),
                grad_block,
                preferred_element_type=jnp.float32,
            )
            row_inner = jnp.sum(probabilities * grad_softmax, axis=-1, keepdims=True)
            grad_scores = (probabilities * (grad_softmax - row_inner)).astype(jnp.bfloat16)
            grad_query_block = (
                jnp.einsum(
                    "hqk,khd->qhd", grad_scores, key_rows, preferred_element_type=jnp.float32
                )
                * score_scale
            )
            key_sum = (
                key_sum
                + jnp.einsum(
                    "hqk,qhd->khd", grad_scores, query_block, preferred_element_type=jnp.float32
                )
                * score_scale
            )
            return ((key_sum, value_sum), grad_query_block)

        zero_heads = jnp.zeros((length, local_heads, HD), jnp.float32)
        (grad_key_rot, grad_value_rows), grad_query_blocks = lax.scan(
            attend_backward,
            (zero_heads, zero_heads),
            (query_blocks, segment_blocks, log_totals, grad_attended),
        )
        grad_query_low = (
            rotate(grad_query_blocks.reshape(length, local_heads, HD), cos_table, -sine_table)
            .astype(jnp.bfloat16)
            .reshape(length, local_width)
        )
        grad_key_low = (
            rotate(grad_key_rot, cos_table, -sine_table)
            .astype(jnp.bfloat16)
            .reshape(length, local_width)
        )
        grad_value_low = grad_value_rows.astype(jnp.bfloat16).reshape(length, local_width)
        query_part = times_transpose(grad_query_low, query_full)
        key_part = times_transpose(grad_key_low, key_full)
        value_part = times_transpose(grad_value_low, value_full)
        grad_input = grad_first_sum + lax.psum_scatter(
            (query_part + key_part + value_part).astype(jnp.bfloat16),
            "tensor",
            scatter_dimension=0,
            tiled=True,
        ).astype(jnp.float32)
        row_grads = (
            contract_rows(full_input, grad_query_low),
            contract_rows(full_input, grad_key_low),
            contract_rows(full_input, grad_value_low),
            grad_gate,
            grad_up,
        )
        col_grads = (grad_output, grad_down)
        norm_parts = (grad_first_gain, grad_first_bias, grad_second_gain, grad_second_bias)
        return (
            layer_output.astype(jnp.bfloat16),
            grad_input.astype(jnp.bfloat16),
            (row_grads, col_grads, norm_parts),
        )

    norm_zero = tuple(
        (
            jnp.zeros(gain_like.shape, jnp.float32)
            for gain_like in (first_gain, first_bias, second_gain, second_bias)
        )
    )
    row_zero = tuple(
        (
            jnp.zeros((model_width, weight_part.shape[1]), jnp.float32)
            for weight_part in (query_weight, key_weight, value_weight, gate_weight, up_weight)
        )
    )
    col_zero = (
        jnp.zeros((output_weight.shape[0], model_width), jnp.float32),
        jnp.zeros((down_weight.shape[0], model_width), jnp.float32),
    )

    def scan_step(totals, batch_rows):
        weights = fetch_weights()
        layer_output, grad_input, grad_terms = micro_step(
            weights, batch_rows[0], batch_rows[1], batch_rows[2]
        )
        return (jax.tree.map(jnp.add, totals, grad_terms), (layer_output, grad_input))

    totals, (outputs, grad_inputs) = lax.scan(
        scan_step, (row_zero, col_zero, norm_zero), (layer_input, cotangent, segment_ids)
    )
    row_grads, col_grads, norm_parts = totals
    row_done = lax.psum_scatter(row_grads, "dp", scatter_dimension=0, tiled=True)
    col_done = (
        lax.psum_scatter(col_grads[0], "dp", scatter_dimension=1, tiled=True),
        lax.psum_scatter(col_grads[1], "dp", scatter_dimension=1, tiled=True),
    )
    norm_done = lax.psum(norm_parts, ("dp", "tensor"))
    totals = (tuple(row_done), tuple(col_done), tuple(norm_done))
    row_done, col_done, norm_done = totals
    return (
        outputs,
        grad_inputs,
        row_done[0],
        row_done[1],
        row_done[2],
        col_done[0],
        row_done[3],
        row_done[4],
        col_done[1],
        norm_done[0],
        norm_done[1],
        norm_done[2],
        norm_done[3],
    )


def solution(mesh):
    in_specs = (
        P("dp", "tensor", None),
        P("dp", "tensor", None),
        P("dp", None),
        P("dp", "tensor"),
        P("dp", "tensor"),
        P("dp", "tensor"),
        P("tensor", "dp"),
        P("dp", "tensor"),
        P("dp", "tensor"),
        P("tensor", "dp"),
        P(),
        P(),
        P(),
        P(),
    )
    out_specs = (
        P("dp", "tensor", None),
        P("dp", "tensor", None),
        P("dp", "tensor"),
        P("dp", "tensor"),
        P("dp", "tensor"),
        P("tensor", "dp"),
        P("dp", "tensor"),
        P("dp", "tensor"),
        P("tensor", "dp"),
        P(),
        P(),
        P(),
        P(),
    )
    return jax.shard_map(
        per_device, mesh=mesh, in_specs=in_specs, out_specs=out_specs, check_vma=False
    )
```

profile of v0, /device:TPU:0, one launch (start us, length us, event | category | flops | bytes accessed | tf_op | source)
XLA Modules:
  0.0 1512.6 jit_solution(8653085761068801146)
XLA Ops:
  9.7 1015.2 %while.85 = (s32[]{:T(128)}, f32[768,192]{0,1:T(8,128)}, f32[768,192]{0,1:T(8,128)}, f32[768,192]{0,1:T(8,128)}, f32[768,768]{1,0:T(8,128)}, /*index=5*/f32[768,...) while((s32[]{:T(128)}, f32[768,192]{0,1:T(8,128)}, ...), condition=%wide.region_24.25_spmd.clone.clone.clone.clone, body=%wide.region_0.24_spmd.clone.clone.clone.clone.sunk | while | flops 15999043584 | bytes 421072320 | solution.py:292
  13.5 33.2 %all_gather.98 = bf16[192,768]{0,1:T(8,128)(2,1)S(1)} all-gather(bf16[192,96]{0,1:T(8,128)(2,1)} %get-tuple-element.1606), channel_id=1, replica_groups=mesh['dp'=8,'tensor'=4] {'dp'}, dimensions={1}, use_global_device_ids=true | all-gather | bytes 331776 | tf_op jit(solution)/shard_map/while/body/eval_jaxpr/all_gather | solution.py:93
  46.6 31.4 %all_gather.97 = bf16[768,192]{1,0:T(8,128)(2,1)S(1)} all-gather(bf16[96,192]{1,0:T(8,128)(2,1)} %get-tuple-element.1603), channel_id=1, replica_groups=mesh['dp'=8,'tensor'=4] {'dp'}, dimensions={0}, use_global_device_ids=true | all-gather | bytes 331776 | tf_op jit(solution)/shard_map/while/body/eval_jaxpr/all_gather | solution.py:88
  78.1 31.3 %all_gather.95 = bf16[768,192]{1,0:T(8,128)(2,1)S(1)} all-gather(bf16[96,192]{1,0:T(8,128)(2,1)} %get-tuple-element.1602), channel_id=1, replica_groups=mesh['dp'=8,'tensor'=4] {'dp'}, dimensions={0}, use_global_device_ids=true | all-gather | bytes 331776 | tf_op jit(solution)/shard_map/while/body/eval_jaxpr/all_gather | solution.py:87
  109.4 31.0 %all_gather.96 = bf16[768,192]{1,0:T(8,128)(2,1)S(1)} all-gather(bf16[96,192]{1,0:T(8,128)(2,1)S(1)} %copy-done.33), channel_id=1, replica_groups=mesh['dp'=8,'tensor'=4] {'dp'}, dimensions={0}, use_global_device_ids=true | all-gather | bytes 331776 | tf_op jit(solution)/shard_map/while/body/eval_jaxpr/all_gather | solution.py:86
  145.7 12.8 while.86
  161.5 28.5 %reduce-scatter.28.cloned.1.call-done = bf16[256,768]{1,0:T(8,128)(2,1)} async-done(((bf16[1024,768]{1,0:T(8,128)(2,1)}), bf16[256,768]{1,0:T(8,128)(2,1)}) %reduce-scatter.28.cloned.1.call-update) | async-done | bytes 393232 | tf_op jit(solution)/shard_map/while/body/eval_jaxpr/reduce_scatter | solution.py:140
  196.5 9.4 all-gather.18.cloned.1.call-done
  205.9 19.5 %all-gather.16.cloned.1.call-done = bf16[1024,768]{1,0:T(8,128)(2,1)} async-done(((bf16[256,768]{1,0:T(8,128)(2,1)}), bf16[1024,768]{1,0:T(8,128)(2,1)}) %all-gather.16.cloned.1.call-update) | async-done | bytes 1572880 | tf_op jit(solution)/shard_map/while/body/eval_jaxpr/all_gather | solution.py:148
  230.2 39.1 %all-gather.20.cloned.1.call-done = bf16[768,768]{1,0:T(8,128)(2,1)} async-done(((bf16[96,768]{1,0:T(8,128)(2,1)}), bf16[768,768]{1,0:T(8,128)(2,1)}) %all-gather.20.cloned.1.call-update) | async-done | bytes 1179664 | tf_op jit(solution)/shard_map/while/body/eval_jaxpr/all_gather | solution.py:90
  269.3 6.4 multiply_convert_fusion.6
  275.7 36.1 %all-gather.22.cloned.1.call-done = bf16[768,768]{0,1:T(8,128)(2,1)} async-done(((bf16[768,96]{0,1:T(8,128)(2,1)}), bf16[768,768]{0,1:T(8,128)(2,1)}) %all-gather.22.cloned.1.call-update) | async-done | bytes 1179664 | tf_op jit(solution)/shard_map/while/body/eval_jaxpr/all_gather | solution.py:94
  316.2 26.8 %reduce-scatter.30.cloned.1.call-done = bf16[256,768]{1,0:T(8,128)(2,1)} async-done(((bf16[1024,768]{1,0:T(8,128)(2,1)}), bf16[256,768]{1,0:T(8,128)(2,1)}) %reduce-scatter.30.cloned.1.call-update) | async-done | bytes 393232 | tf_op jit(solution)/shard_map/while/body/eval_jaxpr/reduce_scatter | solution.py:155
  349.5 19.6 %all-gather.24.cloned.1.call-done = bf16[1024,768]{1,0:T(8,128)(2,1)} async-done(((bf16[256,768]{1,0:T(8,128)(2,1)}), bf16[1024,768]{1,0:T(8,128)(2,1)}) %all-gather.24.cloned.1.call-update) | async-done | bytes 1572880 | tf_op jit(solution)/shard_map/while/body/eval_jaxpr/all_gather | solution.py:167
  369.1 5.8 multiply_convert_fusion.7
  379.8 28.3 %reduce-scatter.32.cloned.1.call-done = bf16[256,768]{1,0:T(8,128)(2,1)} async-done(((bf16[1024,768]{1,0:T(8,128)(2,1)}), bf16[256,768]{1,0:T(8,128)(2,1)}) %reduce-scatter.32.cloned.1.call-update) | async-done | bytes 393232 | tf_op jit(solution)/shard_map/while/body/eval_jaxpr/reduce_scatter | solution.py:175
  418.1 15.9 %all-gather.26.cloned.1.call-done = bf16[1024,768]{1,0:T(8,128)(2,1)} async-done(((bf16[256,768]{1,0:T(8,128)(2,1)}), bf16[1024,768]{1,0:T(8,128)(2,1)}) %all-gather.26.cloned.1.call-update) | async-done | bytes 1572880 | tf_op jit(solution)/shard_map/while/body/eval_jaxpr/all_gather | solution.py:186
  438.1 40.6 %while.87 = (s32[]{:T(128)}, f32[1024,3,64]{0,2,1:T(8,128)S(1)}, f32[1024,3,64]{0,2,1:T(8,128)}, f32[2,512,3,64]{1,0,3,2:T(2,128)}, bf16[2,512,3,64]{1,3,2,0:T(8...) while((s32[]{:T(128)}, f32[1024,3,64]{0,2,1:T(8,128)S(1)}, ...), condition=%wide.region_18.18_spmd.clone, body=%wide.region_16.17_spmd.clone.sunk | while | flops 1031830016 | bytes 56418472 | solution.py:228
  449.7 8.1 dynamic_update_slice.42
  470.5 8.1 dynamic_update_slice.42
  503.1 11.9 reduce-scatter.34.cloned.1.call-done
  521.1 31.5 %all_gather.98 = bf16[192,768]{0,1:T(8,128)(2,1)S(1)} all-gather(bf16[192,96]{0,1:T(8,128)(2,1)} %get-tuple-element.1606), channel_id=1, replica_groups=mesh['dp'=8,'tensor'=4] {'dp'}, dimensions={1}, use_global_device_ids=true | all-gather | bytes 331776 | tf_op jit(solution)/shard_map/while/body/eval_jaxpr/all_gather | solution.py:93
  552.6 31.4 %all_gather.97 = bf16[768,192]{1,0:T(8,128)(2,1)S(1)} all-gather(bf16[96,192]{1,0:T(8,128)(2,1)} %get-tuple-element.1603), channel_id=1, replica_groups=mesh['dp'=8,'tensor'=4] {'dp'}, dimensions={0}, use_global_device_ids=true | all-gather | bytes 331776 | tf_op jit(solution)/shard_map/while/body/eval_jaxpr/all_gather | solution.py:88
  584.0 31.4 %all_gather.95 = bf16[768,192]{1,0:T(8,128)(2,1)S(1)} all-gather(bf16[96,192]{1,0:T(8,128)(2,1)} %get-tuple-element.1602), channel_id=1, replica_groups=mesh['dp'=8,'tensor'=4] {'dp'}, dimensions={0}, use_global_device_ids=true | all-gather | bytes 331776 | tf_op jit(solution)/shard_map/while/body/eval_jaxpr/all_gather | solution.py:87
  615.5 31.0 %all_gather.96 = bf16[768,192]{1,0:T(8,128)(2,1)S(1)} all-gather(bf16[96,192]{1,0:T(8,128)(2,1)S(1)} %copy-done.33), channel_id=1, replica_groups=mesh['dp'=8,'tensor'=4] {'dp'}, dimensions={0}, use_global_device_ids=true | all-gather | bytes 331776 | tf_op jit(solution)/shard_map/while/body/eval_jaxpr/all_gather | solution.py:86
  651.8 12.8 while.86
  667.6 27.6 %reduce-scatter.28.cloned.1.call-done = bf16[256,768]{1,0:T(8,128)(2,1)} async-done(((bf16[1024,768]{1,0:T(8,128)(2,1)}), bf16[256,768]{1,0:T(8,128)(2,1)}) %reduce-scatter.28.cloned.1.call-update) | async-done | bytes 393232 | tf_op jit(solution)/shard_map/while/body/eval_jaxpr/reduce_scatter | solution.py:140
  701.2 9.8 all-gather.18.cloned.1.call-done
  711.0 19.5 %all-gather.16.cloned.1.call-done = bf16[1024,768]{1,0:T(8,128)(2,1)} async-done(((bf16[256,768]{1,0:T(8,128)(2,1)}), bf16[1024,768]{1,0:T(8,128)(2,1)}) %all-gather.16.cloned.1.call-update) | async-done | bytes 1572880 | tf_op jit(solution)/shard_map/while/body/eval_jaxpr/all_gather | solution.py:148
  735.3 39.1 %all-gather.20.cloned.1.call-done = bf16[768,768]{1,0:T(8,128)(2,1)} async-done(((bf16[96,768]{1,0:T(8,128)(2,1)}), bf16[768,768]{1,0:T(8,128)(2,1)}) %all-gather.20.cloned.1.call-update) | async-done | bytes 1179664 | tf_op jit(solution)/shard_map/while/body/eval_jaxpr/all_gather | solution.py:90
  774.4 6.4 multiply_convert_fusion.6
  780.8 36.1 %all-gather.22.cloned.1.call-done = bf16[768,768]{0,1:T(8,128)(2,1)} async-done(((bf16[768,96]{0,1:T(8,128)(2,1)}), bf16[768,768]{0,1:T(8,128)(2,1)}) %all-gather.22.cloned.1.call-update) | async-done | bytes 1179664 | tf_op jit(solution)/shard_map/while/body/eval_jaxpr/all_gather | solution.py:94
  821.3 26.8 %reduce-scatter.30.cloned.1.call-done = bf16[256,768]{1,0:T(8,128)(2,1)} async-done(((bf16[1024,768]{1,0:T(8,128)(2,1)}), bf16[256,768]{1,0:T(8,128)(2,1)}) %reduce-scatter.30.cloned.1.call-update) | async-done | bytes 393232 | tf_op jit(solution)/shard_map/while/body/eval_jaxpr/reduce_scatter | solution.py:155
  854.6 19.6 %all-gather.24.cloned.1.call-done = bf16[1024,768]{1,0:T(8,128)(2,1)} async-done(((bf16[256,768]{1,0:T(8,128)(2,1)}), bf16[1024,768]{1,0:T(8,128)(2,1)}) %all-gather.24.cloned.1.call-update) | async-done | bytes 1572880 | tf_op jit(solution)/shard_map/while/body/eval_jaxpr/all_gather | solution.py:167
  884.9 28.3 %reduce-scatter.32.cloned.1.call-done = bf16[256,768]{1,0:T(8,128)(2,1)} async-done(((bf16[1024,768]{1,0:T(8,128)(2,1)}), bf16[256,768]{1,0:T(8,128)(2,1)}) %reduce-scatter.32.cloned.1.call-update) | async-done | bytes 393232 | tf_op jit(solution)/shard_map/while/body/eval_jaxpr/reduce_scatter | solution.py:175
  923.9 15.2 %all-gather.26.cloned.1.call-done = bf16[1024,768]{1,0:T(8,128)(2,1)} async-done(((bf16[256,768]{1,0:T(8,128)(2,1)}), bf16[1024,768]{1,0:T(8,128)(2,1)}) %all-gather.26.cloned.1.call-update) | async-done | bytes 1572880 | tf_op jit(solution)/shard_map/while/body/eval_jaxpr/all_gather | solution.py:186
  943.2 40.8 %while.87 = (s32[]{:T(128)}, f32[1024,3,64]{0,2,1:T(8,128)S(1)}, f32[1024,3,64]{0,2,1:T(8,128)}, f32[2,512,3,64]{1,0,3,2:T(2,128)}, bf16[2,512,3,64]{1,3,2,0:T(8...) while((s32[]{:T(128)}, f32[1024,3,64]{0,2,1:T(8,128)S(1)}, ...), condition=%wide.region_18.18_spmd.clone, body=%wide.region_16.17_spmd.clone.sunk | while | flops 1031830016 | bytes 56418472 | solution.py:228
  954.8 8.1 dynamic_update_slice.42
  975.5 8.1 dynamic_update_slice.42
  1010.5 9.7 reduce-scatter.34.cloned.1.call-done
  1036.5 39.7 %all-reduce = (f32[768]{0:T(1024)}, f32[768]{0:T(1024)}, f32[768]{0:T(1024)}, f32[768]{0:T(1024)}) all-reduce(f32[768]{0:T(1024)S(1)} %copy-done.58, f32[768]{0:T(1024)S(1)} %copy-done.55, f32[768]{0:T(1024)S(1)} %copy-done.52, f32[768]{0:T(1024)S(1)} %copy-done.49), channel_id=1, replica_groups=mesh['dp'=8,'tensor'=4] {'dp','tensor'}, use_global_device_ids=true, to_apply=%region_32.33 | all-reduce | flops 3072 | bytes 24576 | tf_op jit(solution)/shard_map/psum | solution.py:301
  1076.2 15.0 reduce-scatter.26.cloned.1.call-done
  1092.9 64.2 %reduce-scatter.14.cloned.1.call-done = f32[96,192]{1,0:T(8,128)} async-done(((f32[768,192]{1,0:T(8,128)}), f32[96,192]{1,0:T(8,128)}) %reduce-scatter.14.cloned.1.call-update) | async-done | bytes 73744 | tf_op jit(solution)/shard_map/reduce_scatter | solution.py:296
  1157.0 65.5 %reduce-scatter.16.cloned.1.call-done = f32[96,192]{1,0:T(8,128)} async-done(((f32[768,192]{1,0:T(8,128)}), f32[96,192]{1,0:T(8,128)}) %reduce-scatter.16.cloned.1.call-update) | async-done | bytes 73744 | tf_op jit(solution)/shard_map/reduce_scatter | solution.py:296
  1222.5 65.8 %reduce-scatter.18.cloned.1.call-done = f32[96,192]{1,0:T(8,128)} async-done(((f32[768,192]{1,0:T(8,128)}), f32[96,192]{1,0:T(8,128)}) %reduce-scatter.18.cloned.1.call-update) | async-done | bytes 73744 | tf_op jit(solution)/shard_map/reduce_scatter | solution.py:296
  1288.3 72.1 %reduce-scatter.20.cloned.1.call-done = f32[96,768]{1,0:T(8,128)} async-done(((f32[768,768]{1,0:T(8,128)}), f32[96,768]{1,0:T(8,128)}) %reduce-scatter.20.cloned.1.call-update) | async-done | bytes 294928 | tf_op jit(solution)/shard_map/reduce_scatter | solution.py:296
  1360.4 72.3 %reduce-scatter.22.cloned.1.call-done = f32[96,768]{1,0:T(8,128)} async-done(((f32[768,768]{1,0:T(8,128)}), f32[96,768]{1,0:T(8,128)}) %reduce-scatter.22.cloned.1.call-update) | async-done | bytes 294928 | tf_op jit(solution)/shard_map/reduce_scatter | solution.py:296
  1432.7 72.0 %reduce-scatter.24.cloned.1.call-done = f32[768,96]{0,1:T(8,128)} async-done(((f32[768,768]{0,1:T(8,128)}), f32[768,96]{0,1:T(8,128)}) %reduce-scatter.24.cloned.1.call-update) | async-done | bytes 294928 | tf_op jit(solution)/shard_map/reduce_scatter | solution.py:299
  (542 shorter events, 254.2 us)
Async XLA Ops:
  9.7 134.1 %copy-start.60 = (f32[32]{0:T(128)}, f32[32]{0:T(128)S(1)}, u32[]{:S(2)}) copy-start(f32[32]{0:T(128)S(1)} %get-tuple-element.1613) | copy-start | bytes 388 | tf_op jit(solution)/shard_map/while
  9.7 99.7 %copy-start.33 = (bf16[96,192]{1,0:T(8,128)(2,1)S(1)}, bf16[96,192]{1,0:T(8,128)(2,1)}, u32[]{:S(2)}) copy-start(bf16[96,192]{1,0:T(8,128)(2,1)} %get-tuple-element.1600) | copy-start | bytes 110596 | tf_op jit(solution)/shard_map/while
  9.7 131.9 %all-gather.14.cloned.1.call-start = ((), (), s32[]{:S(2)}) async-start(), calls=%async_computation.18 | async-start | bytes 1966080 | tf_op jit(solution)/shard_map/while/body/eval_jaxpr/all_gather | solution.py:100
  11.5 178.5 %reduce-scatter.28.cloned.1.call-start = ((), (), s32[]{:S(2)}) async-start(), calls=%async_computation.19 | async-start | bytes 1966080 | tf_op jit(solution)/shard_map/while/body/eval_jaxpr/reduce_scatter | solution.py:140
  78.1 66.8 %copy-start.7 = (bf16[768,192]{1,0:T(8,128)(2,1)}, bf16[768,192]{1,0:T(8,128)(2,1)S(1)}, u32[]{:S(2)}) copy-start(bf16[768,192]{1,0:T(8,128)(2,1)S(1)} %all_gather.97) | copy-start | bytes 884740 | tf_op jit(solution)/shard_map/while
  109.4 35.1 %copy-start.11 = (bf16[768,192]{1,0:T(8,128)(2,1)}, bf16[768,192]{1,0:T(8,128)(2,1)S(1)}, u32[]{:S(2)}) copy-start(bf16[768,192]{1,0:T(8,128)(2,1)S(1)} %all_gather.95) | copy-start | bytes 884740 | tf_op jit(solution)/shard_map/while
  159.0 32.2 %copy-start.9 = (bf16[24,8,2,512]{3,1,2,0:T(8,128)(2,1)}, bf16[24,8,2,512]{3,1,2,0:T(8,128)(2,1)S(1)}, u32[]{:S(2)}) copy-start(bf16[24,8,2,512]{3,1,2,0:T(8,128)(2,1)S(1)} %copy.84) | copy-start | bytes 1179652 | tf_op jit(solution)/shard_map/while
  159.0 33.5 %copy-start.32 = (f32[768]{0:T(1024)S(1)}, f32[768]{0:T(1024)}, u32[]{:S(2)}) copy-start(f32[768]{0:T(1024)} %get-tuple-element.1607) | copy-start | bytes 9220 | tf_op jit(solution)/shard_map/while
  159.0 33.5 %copy-start.39 = (f32[768]{0:T(1024)S(1)}, f32[768]{0:T(1024)}, u32[]{:S(2)}) copy-start(f32[768]{0:T(1024)} %get-tuple-element.1608) | copy-start | bytes 9220 | tf_op jit(solution)/shard_map/while
  160.9 45.1 %all-gather.18.cloned.1.call-start = ((), (), s32[]{:S(2)}) async-start(), calls=%async_computation.21 | async-start | bytes 1327104 | tf_op jit(solution)/shard_map/while/body/eval_jaxpr/all_gather | solution.py:89
  161.4 64.0 %all-gather.16.cloned.1.call-start = ((), (), s32[]{:S(2)}) async-start(), calls=%async_computation.20 | async-start | bytes 1966080 | tf_op jit(solution)/shard_map/while/body/eval_jaxpr/all_gather | solution.py:148
  191.2 39.0 %copy-start.35 = (f32[256]{0:T(256)}, f32[256]{0:T(256)S(1)}, u32[]{:S(2)}) copy-start(f32[256]{0:T(256)S(1)} %broadcast_multiply_fusion.4) | copy-start | bytes 3076 | tf_op jit(solution)/shard_map/while
  192.5 37.7 %copy-start.46 = (f32[256]{0:T(256)}, f32[256]{0:T(256)S(1)}, u32[]{:S(2)}) copy-start(f32[256]{0:T(256)S(1)} %multiply_reduce_fusion.9) | copy-start | bytes 3076 | tf_op jit(solution)/shard_map/while
  192.5 37.7 %copy-start.38 = (f32[256]{0:T(256)}, f32[256]{0:T(256)S(1)}, u32[]{:S(2)}) copy-start(f32[256]{0:T(256)S(1)} %fusion.273) | copy-start | bytes 3076 | tf_op jit(solution)/shard_map/while
  194.5 74.7 %all-gather.20.cloned.1.call-start = ((), (), s32[]{:S(2)}) async-start(), calls=%async_computation.22 | async-start | bytes 1327104 | tf_op jit(solution)/shard_map/while/body/eval_jaxpr/all_gather | solution.py:90
  195.1 116.6 %all-gather.22.cloned.1.call-start = ((), (), s32[]{:S(2)}) async-start(), calls=%async_computation.23 | async-start | bytes 1327104 | tf_op jit(solution)/shard_map/while/body/eval_jaxpr/all_gather | solution.py:94
  195.9 147.1 %reduce-scatter.30.cloned.1.call-start = ((), (), s32[]{:S(2)}) async-start(), calls=%async_computation.24 | async-start | bytes 1966080 | tf_op jit(solution)/shard_map/while/body/eval_jaxpr/reduce_scatter | solution.py:155
  316.2 52.9 %all-gather.24.cloned.1.call-start = ((), (), s32[]{:S(2)}) async-start(), calls=%async_computation.25 | async-start | bytes 1966080 | tf_op jit(solution)/shard_map/while/body/eval_jaxpr/all_gather | solution.py:167
  349.5 58.6 %reduce-scatter.32.cloned.1.call-start = ((), (), s32[]{:S(2)}) async-start(), calls=%async_computation.26 | async-start | bytes 1966080 | tf_op jit(solution)/shard_map/while/body/eval_jaxpr/reduce_scatter | solution.py:175
  379.7 54.2 %all-gather.26.cloned.1.call-start = ((), (), s32[]{:S(2)}) async-start(), calls=%async_computation.27 | async-start | bytes 1966080 | tf_op jit(solution)/shard_map/while/body/eval_jaxpr/all_gather | solution.py:186
  414.4 100.6 %reduce-scatter.34.cloned.1.call-start = ((), (), s32[]{:S(2)}) async-start(), calls=%async_computation.28 | async-start | bytes 1966080 | tf_op jit(solution)/shard_map/while/body/eval_jaxpr/reduce_scatter | solution.py:247
  517.3 132.5 %copy-start.60 = (f32[32]{0:T(128)}, f32[32]{0:T(128)S(1)}, u32[]{:S(2)}) copy-start(f32[32]{0:T(128)S(1)} %get-tuple-element.1613) | copy-start | bytes 388 | tf_op jit(solution)/shard_map/while
  517.3 98.2 %copy-start.33 = (bf16[96,192]{1,0:T(8,128)(2,1)S(1)}, bf16[96,192]{1,0:T(8,128)(2,1)}, u32[]{:S(2)}) copy-start(bf16[96,192]{1,0:T(8,128)(2,1)} %get-tuple-element.1600) | copy-start | bytes 110596 | tf_op jit(solution)/shard_map/while
  517.3 130.3 %all-gather.14.cloned.1.call-start = ((), (), s32[]{:S(2)}) async-start(), calls=%async_computation.18 | async-start | bytes 1966080 | tf_op jit(solution)/shard_map/while/body/eval_jaxpr/all_gather | solution.py:100
  519.2 176.0 %reduce-scatter.28.cloned.1.call-start = ((), (), s32[]{:S(2)}) async-start(), calls=%async_computation.19 | async-start | bytes 1966080 | tf_op jit(solution)/shard_map/while/body/eval_jaxpr/reduce_scatter | solution.py:140
  584.0 66.9 %copy-start.7 = (bf16[768,192]{1,0:T(8,128)(2,1)}, bf16[768,192]{1,0:T(8,128)(2,1)S(1)}, u32[]{:S(2)}) copy-start(bf16[768,192]{1,0:T(8,128)(2,1)S(1)} %all_gather.97) | copy-start | bytes 884740 | tf_op jit(solution)/shard_map/while
  615.5 35.1 %copy-start.11 = (bf16[768,192]{1,0:T(8,128)(2,1)}, bf16[768,192]{1,0:T(8,128)(2,1)S(1)}, u32[]{:S(2)}) copy-start(bf16[768,192]{1,0:T(8,128)(2,1)S(1)} %all_gather.95) | copy-start | bytes 884740 | tf_op jit(solution)/shard_map/while
  665.1 32.6 %copy-start.32 = (f32[768]{0:T(1024)S(1)}, f32[768]{0:T(1024)}, u32[]{:S(2)}) copy-start(f32[768]{0:T(1024)} %get-tuple-element.1607) | copy-start | bytes 9220 | tf_op jit(solution)/shard_map/while
  665.1 32.6 %copy-start.39 = (f32[768]{0:T(1024)S(1)}, f32[768]{0:T(1024)}, u32[]{:S(2)}) copy-start(f32[768]{0:T(1024)} %get-tuple-element.1608) | copy-start | bytes 9220 | tf_op jit(solution)/shard_map/while
  666.9 44.1 %all-gather.18.cloned.1.call-start = ((), (), s32[]{:S(2)}) async-start(), calls=%async_computation.21 | async-start | bytes 1327104 | tf_op jit(solution)/shard_map/while/body/eval_jaxpr/all_gather | solution.py:89
  667.5 63.0 %all-gather.16.cloned.1.call-start = ((), (), s32[]{:S(2)}) async-start(), calls=%async_computation.20 | async-start | bytes 1966080 | tf_op jit(solution)/shard_map/while/body/eval_jaxpr/all_gather | solution.py:148
  696.4 38.9 %copy-start.35 = (f32[256]{0:T(256)}, f32[256]{0:T(256)S(1)}, u32[]{:S(2)}) copy-start(f32[256]{0:T(256)S(1)} %broadcast_multiply_fusion.4) | copy-start | bytes 3076 | tf_op jit(solution)/shard_map/while
  697.6 37.7 %copy-start.46 = (f32[256]{0:T(256)}, f32[256]{0:T(256)S(1)}, u32[]{:S(2)}) copy-start(f32[256]{0:T(256)S(1)} %multiply_reduce_fusion.9) | copy-start | bytes 3076 | tf_op jit(solution)/shard_map/while
  697.6 37.7 %copy-start.38 = (f32[256]{0:T(256)}, f32[256]{0:T(256)S(1)}, u32[]{:S(2)}) copy-start(f32[256]{0:T(256)S(1)} %fusion.273) | copy-start | bytes 3076 | tf_op jit(solution)/shard_map/while
  699.7 74.7 %all-gather.20.cloned.1.call-start = ((), (), s32[]{:S(2)}) async-start(), calls=%async_computation.22 | async-start | bytes 1327104 | tf_op jit(solution)/shard_map/while/body/eval_jaxpr/all_gather | solution.py:90
  700.3 116.6 %all-gather.22.cloned.1.call-start = ((), (), s32[]{:S(2)}) async-start(), calls=%async_computation.23 | async-start | bytes 1327104 | tf_op jit(solution)/shard_map/while/body/eval_jaxpr/all_gather | solution.py:94
  701.0 147.1 %reduce-scatter.30.cloned.1.call-start = ((), (), s32[]{:S(2)}) async-start(), calls=%async_computation.24 | async-start | bytes 1966080 | tf_op jit(solution)/shard_map/while/body/eval_jaxpr/reduce_scatter | solution.py:155
  821.3 52.9 %all-gather.24.cloned.1.call-start = ((), (), s32[]{:S(2)}) async-start(), calls=%async_computation.25 | async-start | bytes 1966080 | tf_op jit(solution)/shard_map/while/body/eval_jaxpr/all_gather | solution.py:167
  854.6 58.6 %reduce-scatter.32.cloned.1.call-start = ((), (), s32[]{:S(2)}) async-start(), calls=%async_computation.26 | async-start | bytes 1966080 | tf_op jit(solution)/shard_map/while/body/eval_jaxpr/reduce_scatter | solution.py:175
  884.8 54.2 %all-gather.26.cloned.1.call-start = ((), (), s32[]{:S(2)}) async-start(), calls=%async_computation.27 | async-start | bytes 1966080 | tf_op jit(solution)/shard_map/while/body/eval_jaxpr/all_gather | solution.py:186
  919.4 100.8 %reduce-scatter.34.cloned.1.call-start = ((), (), s32[]{:S(2)}) async-start(), calls=%async_computation.28 | async-start | bytes 1966080 | tf_op jit(solution)/shard_map/while/body/eval_jaxpr/reduce_scatter | solution.py:247
  1024.9 66.4 %reduce-scatter.26.cloned.1.call-start = ((), (), s32[]{:S(2)}) async-start(), calls=%async_computation.17 | async-start | bytes 884736
  1027.2 129.8 %reduce-scatter.14.cloned.1.call-start = ((), (), s32[]{:S(2)}) async-start(), calls=%async_computation.11 | async-start | bytes 884736 | tf_op jit(solution)/shard_map/reduce_scatter | solution.py:296
  1029.6 192.9 %reduce-scatter.16.cloned.1.call-start = ((), (), s32[]{:S(2)}) async-start(), calls=%async_computation.12 | async-start | bytes 884736 | tf_op jit(solution)/shard_map/reduce_scatter | solution.py:296
  1030.9 257.5 %reduce-scatter.18.cloned.1.call-start = ((), (), s32[]{:S(2)}) async-start(), calls=%async_computation.13 | async-start | bytes 884736 | tf_op jit(solution)/shard_map/reduce_scatter | solution.py:296
  1032.1 328.3 %reduce-scatter.20.cloned.1.call-start = ((), (), s32[]{:S(2)}) async-start(), calls=%async_computation.14 | async-start | bytes 2654208 | tf_op jit(solution)/shard_map/reduce_scatter | solution.py:296
  1032.9 399.8 %reduce-scatter.22.cloned.1.call-start = ((), (), s32[]{:S(2)}) async-start(), calls=%async_computation.15 | async-start | bytes 2654208 | tf_op jit(solution)/shard_map/reduce_scatter | solution.py:296
  1033.6 471.1 %reduce-scatter.24.cloned.1.call-start = ((), (), s32[]{:S(2)}) async-start(), calls=%async_computation.16 | async-start | bytes 2654208 | tf_op jit(solution)/shard_map/reduce_scatter | solution.py:299
  (112 other events, 568.7 us)
Sparse Core Ops, SparseCore 0:
  12.1 22.3 all-gather.13
  161.0 29.0 reduce-scatter.27
  316.3 26.6 reduce-scatter.29
  379.9 28.1 reduce-scatter.31
  486.8 28.1 reduce-scatter.33
  519.4 19.6 all-gather.13
  667.0 28.0 reduce-scatter.27
  821.4 26.6 reduce-scatter.29
  884.9 28.1 reduce-scatter.31
  992.0 28.1 reduce-scatter.33
Sparse Core Ops, SparseCore 1:
  163.5 42.3 all-gather.17
  207.4 18.0 all-gather.15
  227.7 41.5 all-gather.19
  271.7 40.0 all-gather.21
  349.5 19.5 all-gather.23
  414.5 19.5 all-gather.25
  669.6 41.4 all-gather.17
  712.5 18.0 all-gather.15
  732.8 41.5 all-gather.19
  776.8 40.0 all-gather.21
  854.6 19.5 all-gather.23
  919.5 19.5 all-gather.25
  1028.6 62.5 reduce-scatter.25
  1095.5 61.5 reduce-scatter.13
  1160.9 61.5 reduce-scatter.15
  1226.7 61.5 reduce-scatter.17
  1292.4 67.9 reduce-scatter.19
  1364.5 68.1 reduce-scatter.21
  1436.6 68.0 reduce-scatter.23
where the time goes:
time: 1520 us; the launch traced here: 1510 us
  waiting for transfers between devices  899 us (59%)
  blocking collectives  292 us (19%)
  matrix products  147 us (10%)
  local copies, waits for them, and re-layouts  78.3 us (5%)
  other arithmetic  72.1 us (5%)
  between operations  16.1 us (1%)
    reduce_scatter x5, waiting for transfers between devices, per_device(): lax.psum_scatter(row_grads, 'dp', scatter_dimension=0, tiled=True)  340 us
    all_gather x2, waiting for transfers between devices, fetch_weights(): lax.all_gather(up_weight, 'dp', axis=0, tiled=True)  78.1 us
    all_gather x2, waiting for transfers between devices, fetch_weights(): lax.all_gather(down_weight, 'dp', axis=1, tiled=True)  72.2 us
    reduce_scatter x1, waiting for transfers between devices, per_device(): lax.psum_scatter(col_grads[1], 'dp', scatter_dimension=1, tiled=True)  72 us
    all_gather x2, blocking collectives, fetch_weights(): lax.all_gather(output_weight, 'dp', axis=1, tiled=True)  64.6 us
    all_gather x2, blocking collectives, fetch_weights(): lax.all_gather(value_weight, 'dp', axis=0, tiled=True)  62.8 us
    all_gather x2, blocking collectives, fetch_weights(): lax.all_gather(key_weight, 'dp', axis=0, tiled=True)  62.8 us
    all_gather x2, blocking collectives, fetch_weights(): lax.all_gather(query_weight, 'dp', axis=0, tiled=True)  61.9 us
  transfers between devices with their start and end apart: 29, of which 27 were waited for; matrix products, arithmetic and copies ran while one was open for 5% of the time, Pallas kernels for 0%

commit v1 on v0

--- a/solution.py
+++ b/solution.py
@@ -1,6 +1,11 @@
+import functools
+
 import jax
 import jax.numpy as jnp
+import numpy as np
 from jax import lax
+from jax.experimental import pallas as pl
+from jax.experimental.pallas import tpu as pltpu
 from jax.sharding import PartitionSpec as P
 
 HD = 64
@@ -316,6 +321,836 @@
         norm_done[2],
         norm_done[3],
     )
+
+
+F32 = jnp.float32
+BF16 = jnp.bfloat16
+NY = 2
+LANES = 128
+MESH = pl.DeviceIdType.MESH
+
+
+def mm(left, right):
+    return lax.dot_general(left, right, (((1,), (0,)), ((), ())), preferred_element_type=F32)
+
+
+def mt(left, right):
+    return lax.dot_general(left, right, (((1,), (1,)), ((), ())), preferred_element_type=F32)
+
+
+def lane_tables(length):
+    half = HD // 2
+    steps = np.arange(half, dtype=np.float32)
+    frequency = np.float32(rope_base) ** (-(np.float32(2.0) * steps) / np.float32(HD))
+    angles = np.arange(length, dtype=np.float32)[:, None] * frequency[None, :]
+    angles = angles.astype(np.float32)
+    cos, sin = np.cos(angles).astype(np.float32), np.sin(angles).astype(np.float32)
+    cos_lane = np.concatenate([cos] * 4, axis=1)
+    sin_lane = np.concatenate([-sin, sin, -sin, sin], axis=1)
+    return cos_lane, sin_lane, np.ascontiguousarray(cos.T), np.ascontiguousarray(sin.T)
+
+
+def norm_of(v):
+    mu = jnp.mean(v, axis=-1, keepdims=True)
+    cen = v - mu
+    rstd = lax.rsqrt(jnp.mean(cen * cen, axis=-1, keepdims=True) + eps_norm)
+    return cen * rstd, rstd
+
+
+def grad_of_norm(dn, n, rstd):
+    m0 = jnp.mean(dn, axis=-1, keepdims=True)
+    m1 = jnp.mean(dn * n, axis=-1, keepdims=True)
+    return (dn - m0 - n * m1) * rstd
+
+
+def colsum(v):
+    return jnp.sum(v, axis=0, keepdims=True)
+
+
+def layer_kernel(
+    nz,
+    xin,
+    cot,
+    seg,
+    wpk,
+    g1_ref,
+    b1_ref,
+    g2_ref,
+    b2_ref,
+    cosl_h,
+    sinl_h,
+    cosf_h,
+    sinf_h,
+    out_h,
+    gin_h,
+    gw_h,
+    ng_out,
+    W,
+    G,
+    S1X,
+    S1Y,
+    S2X,
+    S2Y,
+    ZR,
+    X,
+    XT,
+    TT,
+    DT,
+    CT,
+    SC,
+    COSL,
+    SINL,
+    COSF,
+    SINF,
+    PK,
+    QZ,
+    KT,
+    VT,
+    LSE,
+    DEL,
+    ATT,
+    ATTT,
+    N1,
+    R1,
+    F4,
+    GP,
+    UP,
+    RR,
+    DZ,
+    CXS,
+    CXR,
+    ACC,
+    OB,
+    DKA,
+    DVA,
+    NG,
+    NR,
+    NS,
+    NZR,
+    loc,
+    ssem,
+    rsem,
+):
+    quarter, width = X.shape[1], X.shape[2]
+    length = 4 * quarter
+    rows = W.shape[4]
+    dp = lax.axis_index("dp")
+    tt = lax.axis_index("tensor")
+    c = lax.rem(tt, 2)
+    xi = lax.div(tt, 2)
+    z = lax.div(dp, NY)
+    y = lax.rem(dp, NY)
+    oy = 1 - y
+    t_x = lax.rem(tt + 2, 4)
+    dev_x = (dp, t_x)
+    dev_c = (dp, tt + 1 - 2 * c)
+    dev_y = (dp + 1 - 2 * y, tt)
+    zs = [lax.rem(z + j, nz) for j in range(nz)]
+    zfrom = [lax.rem(z + nz - j, nz) for j in range(nz)]
+    dev_z = [(zs[j] * NY + y, tt) for j in range(nz)]
+    hz = nz // 2
+    count = [0]
+    lcount = [0]
+    sends = {}
+
+    def rc(src, dst, dev):
+        i = count[0]
+        count[0] += 1
+        copy = pltpu.make_async_remote_copy(
+            src_ref=src,
+            dst_ref=dst,
+            send_sem=ssem.at[i],
+            recv_sem=rsem.at[i],
+            device_id=dev,
+            device_id_type=MESH,
+        )
+        copy.start()
+        sends[id(copy)] = copy
+        return copy
+
+    def sent(copy):
+        copy.wait_send()
+        del sends[id(copy)]
+
+    def lc(src, dst):
+        i = lcount[0]
+        lcount[0] += 1
+        copy = pltpu.make_async_copy(src, dst, loc.at[i])
+        copy.start()
+        return copy
+
+    l_w = lc(wpk, W.at[:, 0, z, y])
+    l_x = lc(xin.at[xi], X.at[tt])
+    l_ct = lc(cot.at[xi], CT.at[xi])
+    l_tab = [lc(cosl_h, COSL), lc(sinl_h, SINL), lc(cosf_h, COSF), lc(sinf_h, SINF)]
+
+    barrier = pltpu.get_barrier_semaphore()
+    peers = [dev_x, dev_c, dev_y] + dev_z[1:]
+    for dev in peers:
+        pl.semaphore_signal(barrier, inc=1, device_id=dev, device_id_type=MESH)
+    pl.semaphore_wait(barrier, len(peers))
+
+    ag = {}
+
+    def e1(k):
+        own = wpk.at[k]
+        ag[k, "z"] = [rc(own, W.at[k, 0, z, y], dev_z[j]) for j in range(1, nz)]
+        ag[k, "x"] = [rc(own, W.at[k, 1, z, y], dev_x)]
+        ag[k, "y"] = [rc(own, W.at[k, 0, z, y], dev_y)]
+
+    def e2(k):
+        for j in range(1, nz):
+            ag[k, "z"][j - 1].wait_recv()
+            part = W.at[k, 0, zfrom[j], y]
+            ag[k, "x"].append(rc(part, W.at[k, 1, zfrom[j], y], dev_x))
+            ag[k, "y"].append(rc(part, part, dev_y))
+
+    def e3(k):
+        ag[k, "d"] = []
+        for j in range(nz):
+            ag[k, "x"][j].wait_recv()
+            if j < hz:
+                part = W.at[k, 1, zfrom[j], y]
+                ag[k, "d"].append(rc(part, part, dev_y))
+            ag[k, "y"][j].wait_recv()
+            if j >= hz:
+                ag[k, "d"].append(rc(W.at[k, 0, zfrom[j], oy], W.at[k, 1, zfrom[j], oy], dev_x))
+
+    def e4(k):
+        for copy in ag[k, "d"]:
+            copy.wait_recv()
+
+    def e_sent(k):
+        for copy in ag[k, "z"] + ag[k, "x"] + ag[k, "y"] + ag[k, "d"]:
+            sent(copy)
+
+    x_far = rc(xin.at[1 - xi], X.at[tt], dev_x)
+    x_core = rc(xin.at[xi], X.at[tt], dev_c)
+    e1(0)
+
+    SC[...] = jnp.broadcast_to(seg[pl.ds(xi, 1), :].astype(F32), (LANES, length)).T
+    NG[...] = jnp.zeros_like(NG)
+    lane = lax.broadcasted_iota(jnp.int32, (1, LANES), 1)
+    low_half = lane < HD
+    swap_low = lax.rem(lane, HD) < (HD // 2)
+
+    def swap(v):
+        return jnp.where(swap_low, pltpu.roll(v, LANES - HD // 2, 1), pltpu.roll(v, HD // 2, 1))
+
+    def at_quarter(i):
+        return pl.ds(pl.multiple_of(i * quarter, quarter), quarter)
+
+    def wmat(k, s, lo=0, hi=None):
+        hi = width if hi is None else hi
+        return W[k, s, :, :, :, lo:hi].reshape(width, hi - lo)
+
+    def turn_rows(src, dst):
+        def step(i, _):
+            dst[:, at_quarter(i)] = src[i].T
+            return 0
+
+        lax.fori_loop(0, 4, step, 0)
+
+    x_far.wait_recv()
+    x_core2 = rc(X.at[t_x], X.at[t_x], dev_c)
+    x_core.wait_recv()
+    l_x.wait()
+    l_w.wait()
+    l_ct.wait()
+    for copy in l_tab:
+        copy.wait()
+    x_core2.wait_recv()
+    turn_rows(X, XT)
+    e2(0)
+    e1(1)
+    ct_far = rc(cot.at[1 - xi], CT.at[xi], dev_x)
+    e3(0)
+    e4(0)
+
+    def project(s):
+        def step(i, _):
+            at = at_quarter(i)
+            y5 = mm(X[i], wmat(0, s, 0, 5 * LANES))
+            cos, sin = COSL[at, :], SINL[at, :]
+            turned = []
+            for b in range(5):
+                v = y5[:, b * LANES : (b + 1) * LANES]
+                if b in (0, 1, 3):
+                    v = v * cos + swap(v) * sin
+                v = v.astype(BF16)
+                PK[s, b, at, :] = v
+                turned.append(v.T)
+            zero = jnp.zeros((HD, quarter), BF16)
+            q0 = turned[0] * BF16(0.125)
+            q2 = turned[3] * BF16(0.125)
+            QZ[3 * s, :HD, at] = q0[:HD]
+            QZ[3 * s, HD:, at] = zero
+            QZ[3 * s + 1, :HD, at] = zero
+            QZ[3 * s + 1, HD:, at] = q0[HD:]
+            QZ[3 * s + 2, :HD, at] = zero
+            QZ[3 * s + 2, HD:, at] = q2[:HD]
+            KT[3 * s, :, at] = turned[1][:HD]
+            KT[3 * s + 1, :, at] = turned[1][HD:]
+            KT[3 * s + 2, :, at] = turned[3][HD:]
+            VT[3 * s, :, at] = turned[2][:HD]
+            VT[3 * s + 1, :, at] = turned[2][HD:]
+            VT[3 * s + 2, :, at] = turned[4][:HD]
+            return 0
+
+        lax.fori_loop(0, 4, step, 0)
+
+    def scores_of(s, hh, h, at):
+        st = mm(PK[s, 1 + 2 * lax.div(hh, 2)], QZ[h, :, at])
+        key_seg = jnp.concatenate([SC[...]] * (quarter // LANES), axis=1)
+        query_seg = seg[pl.ds(xi, 1), at].astype(F32)
+        return jnp.where(key_seg == query_seg, st, mask_fill)
+
+    def attend(s):
+        def step(n, _):
+            hh = lax.div(n, 4)
+            h = 3 * s + hh
+            at = at_quarter(lax.rem(n, 4))
+            st = scores_of(s, hh, h, at)
+            top = jnp.max(st, axis=0, keepdims=True)
+            p = jnp.exp(st - top)
+            total = jnp.sum(p, axis=0, keepdims=True)
+            ot = mm(VT[h], p.astype(BF16)) * (1.0 / total)
+            LSE[h, :, at] = top + jnp.log(total)
+            ATTT[h, :, at] = ot.astype(BF16)
+            return 0
+
+        lax.fori_loop(0, 12, step, 0)
+
+        def turn(i, _):
+            at = at_quarter(i)
+            pair = jnp.concatenate([ATTT[3 * s, :, at], ATTT[3 * s + 1, :, at]], axis=0)
+            lone = jnp.concatenate([jnp.zeros((HD, quarter), BF16), ATTT[3 * s + 2, :, at]], axis=0)
+            ATT[s, at, :LANES] = lone.T
+            ATT[s, at, LANES:] = pair.T
+            return 0
+
+        lax.fori_loop(0, 4, turn, 0)
+
+    project(0)
+    project(1)
+    e2(1)
+    e1(2)
+    attend(0)
+    e3(1)
+    e2(2)
+    e1(3)
+    attend(1)
+
+    last_exchange = []
+
+    def exchange(n, part):
+        if last_exchange:
+            sent(last_exchange.pop())
+
+        def other(k, _):
+            CXS[k] = part(1 - c + 2 * k).astype(BF16)
+            return 0
+
+        lax.fori_loop(0, 2, other, 0)
+        copy = rc(CXS, CXR.at[n % 2], dev_c)
+        last_exchange.append(copy)
+
+        def own(k, _):
+            ACC[k] = part(c + 2 * k)
+            return 0
+
+        lax.fori_loop(0, 2, own, 0)
+        copy.wait_recv()
+
+    def spread():
+        return [rc(F4.at[c + 2 * k], F4.at[c + 2 * k], dev_c) for k in range(2)]
+
+    def out_part(i):
+        at = at_quarter(i)
+        return mt(ATT[0, at, :], wmat(0, 0, 4 * LANES)) + mt(ATT[1, at, :], wmat(0, 1, 4 * LANES))
+
+    exchange(0, out_part)
+    tile = quarter // 2
+
+    def over_tiles(fn):
+        def step(n, _):
+            k = lax.div(n, 2)
+            fn(k, c + 2 * k, pl.ds(pl.multiple_of(lax.rem(n, 2) * tile, tile), tile))
+            return 0
+
+        lax.fori_loop(0, 4, step, 0)
+
+    def first_norm(k, i, at):
+        z1 = X[i, at, :].astype(F32) + ACC[k, at, :] + CXR[0, k, at, :].astype(F32)
+        n1, rstd = norm_of(z1)
+        N1[k, at, :] = n1
+        R1[k, at, :] = jnp.broadcast_to(rstd, (tile, LANES))
+        F4[i, at, :] = (n1 * g1_ref[...] + b1_ref[...]).astype(BF16)
+
+    over_tiles(first_norm)
+    h_copies = spread()
+    e4(1)
+    for copy in h_copies:
+        copy.wait_recv()
+    turn_rows(F4, TT)
+    e3(2)
+    e2(3)
+    e4(2)
+
+    def ff_up(n, _):
+        s = lax.div(n, 4)
+        i = lax.rem(n, 4)
+        at = at_quarter(i)
+        g = mm(F4[i], wmat(1, s))
+        u = mm(F4[i], wmat(2, s))
+        GP[s, at, :] = g.astype(BF16)
+        UP[s, at, :] = u.astype(BF16)
+        RR[s, at, :] = (g * jax.nn.sigmoid(g) * u).astype(BF16)
+        return 0
+
+    lax.fori_loop(0, 8, ff_up, 0)
+    e3(3)
+    e4(3)
+
+    def down_part(i):
+        at = at_quarter(i)
+        return mt(RR[0, at, :], wmat(3, 0)) + mt(RR[1, at, :], wmat(3, 1))
+
+    for copy in h_copies:
+        sent(copy)
+    exchange(1, down_part)
+    ct_far.wait_recv()
+
+    def second_norm(k, i, at):
+        h = N1[k, at, :] * g1_ref[...] + b1_ref[...]
+        z2 = h + ACC[k, at, :] + CXR[1, k, at, :].astype(F32)
+        n2, rstd = norm_of(z2)
+        OB[0, k, at, :] = (n2 * g2_ref[...] + b2_ref[...]).astype(BF16)
+        dy = CT[k, at, :].astype(F32)
+        NG[2:3, :] += colsum(dy * n2)
+        NG[3:4, :] += colsum(dy)
+        dz = grad_of_norm(dy * g2_ref[...], n2, rstd)
+        DZ[k, at, :] = dz
+        F4[i, at, :] = dz.astype(BF16)
+
+    over_tiles(second_norm)
+    d_copies = spread()
+    o_far = rc(OB.at[0, 1 - xi], out_h.at[xi], dev_x)
+    o_own = lc(OB.at[0, xi], out_h.at[xi])
+
+    slots = {3: G, 1: W.at[3], 2: W.at[1], 0: W.at[2]}
+    rs = {}
+    lo_z, hi_z = pl.ds(0, hz), pl.ds(hz, nz - hz)
+
+    def r1(k):
+        g = slots[k]
+        rs[k, "dx"] = rc(g.at[1, lo_z, oy], S1X.at[k], dev_x)
+        rs[k, "dy"] = rc(g.at[1, hi_z, oy], S1Y.at[k], dev_y)
+        rs[k, "x0"] = rc(g.at[1, lo_z, y], S2X.at[k, lo_z], dev_x)
+        rs[k, "y0"] = rc(g.at[0, hi_z, oy], S2Y.at[k, hi_z], dev_y)
+
+    def r2(k):
+        g = slots[k]
+        rs[k, "dx"].wait_recv()
+        for j in range(hz):
+            g[0, j, oy] = (g[0, j, oy].astype(F32) + S1X[k, j].astype(F32)).astype(BF16)
+        rs[k, "y1"] = rc(g.at[0, lo_z, oy], S2Y.at[k, lo_z], dev_y)
+        rs[k, "dy"].wait_recv()
+        for j in range(hz, nz):
+            g[1, j, y] = (g[1, j, y].astype(F32) + S1Y[k, j - hz].astype(F32)).astype(BF16)
+        rs[k, "x1"] = rc(g.at[1, hi_z, y], S2X.at[k, hi_z], dev_x)
+
+    def r3(k):
+        g = slots[k]
+        for name in ("x0", "y0", "y1", "x1"):
+            rs[k, name].wait_recv()
+        for j in range(nz):
+            g[0, j, y] = (
+                g[0, j, y].astype(F32) + S2X[k, j].astype(F32) + S2Y[k, j].astype(F32)
+            ).astype(BF16)
+        rs[k, "z"] = [rc(g.at[0, zs[j], y], ZR.at[k, z], dev_z[j]) for j in range(1, nz)]
+
+    def r4(k):
+        g = slots[k]
+        for copy in rs[k, "z"]:
+            copy.wait_recv()
+        total = g[0, z, y].astype(F32)
+        for j in range(1, nz):
+            total = total + ZR[k, zfrom[j]].astype(F32)
+        place = N1.at[k // 2, pl.ds((k % 2) * rows, rows)]
+        place[...] = total
+        rs[k, "out"] = lc(place, gw_h.at[k])
+
+    def weight_grad(k, left, right):
+        g = slots[k]
+        block = NY * rows
+
+        def step(n, _):
+            s = lax.div(n, nz)
+            j = lax.rem(n, nz)
+            at = pl.ds(pl.multiple_of(j * block, block), block)
+            g[s, j] = mm(left[at, :], right[s]).astype(BF16).reshape(NY, rows, width)
+            return 0
+
+        lax.fori_loop(0, 2 * nz, step, 0)
+
+    for copy in d_copies:
+        copy.wait_recv()
+    turn_rows(F4, DT)
+    weight_grad(3, DT, RR)
+    r1(3)
+
+    def ff_back(n, _):
+        s = lax.div(n, 4)
+        i = lax.rem(n, 4)
+        at = at_quarter(i)
+        dr = mm(F4[i], wmat(3, s))
+        g = GP[s, at, :].astype(F32)
+        u = UP[s, at, :].astype(F32)
+        sg = jax.nn.sigmoid(g)
+        GP[s, at, :] = (dr * u * sg * (1.0 + g * (1.0 - sg))).astype(BF16)
+        UP[s, at, :] = (dr * g * sg).astype(BF16)
+        return 0
+
+    lax.fori_loop(0, 8, ff_back, 0)
+    e_sent(3)
+    weight_grad(1, TT, GP)
+    r1(1)
+    r2(3)
+
+    def hidden_part(i):
+        at = at_quarter(i)
+        return (
+            mt(GP[0, at, :], wmat(1, 0))
+            + mt(UP[0, at, :], wmat(2, 0))
+            + mt(GP[1, at, :], wmat(1, 1))
+            + mt(UP[1, at, :], wmat(2, 1))
+        )
+
+    for copy in d_copies:
+        sent(copy)
+    exchange(2, hidden_part)
+
+    def first_norm_back(k, i, at):
+        dh = DZ[k, at, :] + ACC[k, at, :] + CXR[0, k, at, :].astype(F32)
+        n1 = N1[k, at, :]
+        NG[0:1, :] += colsum(dh * n1)
+        NG[1:2, :] += colsum(dh)
+        dz = grad_of_norm(dh * g1_ref[...], n1, R1[k, at, :1])
+        DZ[k, at, :] = dz
+        F4[i, at, :] = dz.astype(BF16)
+
+    over_tiles(first_norm_back)
+    b_copies = spread()
+    n_core = rc(NG, NR.at[0], dev_c)
+    e_sent(1)
+    e_sent(2)
+    weight_grad(2, TT, UP)
+    r3(3)
+    r1(2)
+    r2(1)
+    for copy in b_copies:
+        copy.wait_recv()
+    n_core.wait_recv()
+    NS[0] = NG[...] + NR[0]
+    n_x = rc(NS.at[0], NR.at[1], dev_x)
+    turn_rows(F4, DT)
+
+    def out_grad(n, _):
+        s = lax.div(n, nz)
+        j = lax.rem(n, nz)
+        block = NY * rows
+        at = pl.ds(pl.multiple_of(j * block, block), block)
+        part = mm(DT[at, :], ATT[s]).astype(BF16)
+        slots[0][s, j, :, :, 4 * LANES :] = part.reshape(NY, rows, 2 * LANES)
+        return 0
+
+    lax.fori_loop(0, 2 * nz, out_grad, 0)
+
+    def head_lanes(h):
+        return pl.ds(pl.multiple_of(h * LANES, LANES), LANES)
+
+    def att_grad(i, _):
+        at = at_quarter(i)
+        for s in range(2):
+            da = mm(F4[i], wmat(0, s, 4 * LANES))
+            pair = da[:, LANES:]
+            lone = pltpu.roll(da[:, :LANES], HD, 1)
+            zero = jnp.zeros_like(pair)
+            views = (
+                jnp.where(low_half, pair, zero),
+                jnp.where(low_half, zero, pair),
+                jnp.where(low_half, lone, zero),
+            )
+            for hh in range(3):
+                h = 3 * s + hh
+                v = views[hh].astype(BF16)
+                GP[0, at, h * LANES : (h + 1) * LANES] = v
+                vt = v.T
+                TT[h * LANES : (h + 1) * LANES, at] = vt
+                part = vt[HD:] if hh == 1 else vt[:HD]
+                DEL[h, :, at] = colsum(part.astype(F32) * ATTT[h, :, at].astype(F32))
+        return 0
+
+    lax.fori_loop(0, 4, att_grad, 0)
+    n_x.wait_recv()
+    NS[1] = NS[0] + NR[1]
+    n_y = rc(NS.at[1], NR.at[2], dev_y)
+    r2(2)
+    r3(1)
+
+    def attend_back(s):
+        def head(hh, _):
+            h = 3 * s + hh
+            DKA[...] = jnp.zeros_like(DKA)
+            DVA[...] = jnp.zeros_like(DVA)
+            hl = head_lanes(h)
+
+            def step(qb, _):
+                at = at_quarter(qb)
+                p = jnp.exp(scores_of(s, hh, h, at) - LSE[h, :, at])
+                dpt = mm(PK[s, 2 + 2 * lax.div(hh, 2)], TT[hl, at])
+                ds = (p * (dpt - DEL[h, :, at])).astype(BF16)
+                DVA[...] += mm(p.astype(BF16), GP[0, at, hl])
+                DKA[...] += mm(ds, PK[s, 3 * lax.div(hh, 2), at, :])
+                dq = mm(KT[h], ds) * 0.125
+                a, b = dq[: HD // 2], dq[HD // 2 :]
+                cos, sin = COSF[:, at], SINF[:, at]
+                VT[h, : HD // 2, at] = (a * cos + b * sin).astype(BF16)
+                VT[h, HD // 2 :, at] = (b * cos - a * sin).astype(BF16)
+                return 0
+
+            lax.fori_loop(0, 4, step, 0)
+
+            def finish(i, _):
+                at = at_quarter(i)
+                dk = DKA[at, :] * 0.125
+                UP[0, at, hl] = (dk * COSL[at, :] - swap(dk) * SINL[at, :]).astype(BF16)
+                GP[0, at, hl] = DVA[at, :].astype(BF16)
+                return 0
+
+            lax.fori_loop(0, 4, finish, 0)
+            return 0
+
+        lax.fori_loop(0, 3, head, 0)
+
+        def gather(i, _):
+            at = at_quarter(i)
+
+            def part(ref, hh):
+                h = 3 * s + hh
+                return ref[0, at, h * LANES : (h + 1) * LANES].astype(F32)
+
+            dq0 = jnp.concatenate([VT[3 * s, :, at], VT[3 * s + 1, :, at]], axis=0).T
+            dq2 = jnp.concatenate([VT[3 * s + 2, :, at]] * 2, axis=0).T
+            dk2 = pltpu.roll(part(UP, 2), HD, 1)
+            dv2 = part(GP, 2)
+            RR[s, at, 0:LANES] = dq0
+            RR[s, at, LANES : 2 * LANES] = jnp.where(low_half, part(UP, 0), part(UP, 1)).astype(BF16)
+            RR[s, at, 2 * LANES : 3 * LANES] = jnp.where(
+                low_half, part(GP, 0), part(GP, 1)
+            ).astype(BF16)
+            RR[s, at, 3 * LANES : 4 * LANES] = jnp.where(low_half, dq2.astype(F32), dk2).astype(BF16)
+            RR[s, at, 4 * LANES : 5 * LANES] = jnp.where(
+                low_half, dv2, jnp.zeros_like(dv2)
+            ).astype(BF16)
+            return 0
+
+        lax.fori_loop(0, 4, gather, 0)
+
+    attend_back(0)
+    r4(3)
+    r3(2)
+    n_y.wait_recv()
+    NS[2] = NS[1] + NR[2]
+    NZR[z] = NS[2]
+    n_z = [rc(NS.at[2], NZR.at[z], dev_z[j]) for j in range(1, nz)]
+    attend_back(1)
+
+    def in_grad(n, _):
+        s = lax.div(n, nz)
+        j = lax.rem(n, nz)
+        block = NY * rows
+        at = pl.ds(pl.multiple_of(j * block, block), block)
+        part = mm(XT[at, :], RR[s, :, : 5 * LANES])
+        mixed = slots[0][s, j, :, :, 4 * LANES : 5 * LANES].reshape(block, LANES)
+        mixed = (part[:, 4 * LANES :] + mixed.astype(F32)).astype(BF16)
+        slots[0][s, j, :, :, : 4 * LANES] = (
+            part[:, : 4 * LANES].astype(BF16).reshape(NY, rows, 4 * LANES)
+        )
+        slots[0][s, j, :, :, 4 * LANES : 5 * LANES] = mixed.reshape(NY, rows, LANES)
+        return 0
+
+    lax.fori_loop(0, 2 * nz, in_grad, 0)
+    r1(0)
+    r4(1)
+
+    def input_part(i):
+        at = at_quarter(i)
+        return mt(RR[0, at, : 5 * LANES], wmat(0, 0, 0, 5 * LANES)) + mt(
+            RR[1, at, : 5 * LANES], wmat(0, 1, 0, 5 * LANES)
+        )
+
+    exchange(3, input_part)
+
+    def input_grad(k, i, at):
+        g = DZ[k, at, :] + ACC[k, at, :] + CXR[1, k, at, :].astype(F32)
+        OB[1, k, at, :] = g.astype(BF16)
+
+    over_tiles(input_grad)
+    i_far = rc(OB.at[1, 1 - xi], gin_h.at[xi], dev_x)
+    i_own = lc(OB.at[1, xi], gin_h.at[xi])
+    r2(0)
+    r4(2)
+    for copy in n_z:
+        copy.wait_recv()
+    total = NZR[0]
+    for j in range(1, nz):
+        total = total + NZR[j]
+    ng_out[...] = total
+    r3(0)
+    r4(0)
+    o_far.wait_recv()
+    i_far.wait_recv()
+    o_own.wait()
+    i_own.wait()
+    for k in range(4):
+        rs[k, "out"].wait()
+    for copy in list(sends.values()):
+        sent(copy)
+
+
+def layer_per_device(
+    dp_size,
+    layer_input,
+    cotangent,
+    segment_ids,
+    query_weight,
+    key_weight,
+    value_weight,
+    output_weight,
+    gate_weight,
+    up_weight,
+    down_weight,
+    first_gain,
+    first_bias,
+    second_gain,
+    second_bias,
+):
+    _, quarter, width = layer_input.shape
+    length = 4 * quarter
+    rows = query_weight.shape[0]
+    nz = dp_size // NY
+    out_turned = output_weight.T
+    two = 2 * HD
+    attention_pack = jnp.concatenate(
+        [
+            query_weight[:, :two],
+            key_weight[:, :two],
+            value_weight[:, :two],
+            query_weight[:, two:],
+            key_weight[:, two:],
+            value_weight[:, two:],
+            out_turned[:, two:],
+            out_turned[:, :two],
+        ],
+        axis=1,
+    )
+    packed = jnp.stack([attention_pack, gate_weight, up_weight, down_weight.T])
+    tables = [jnp.asarray(t) for t in lane_tables(length)]
+    vectors = [v.reshape(1, width) for v in (first_gain, first_bias, second_gain, second_bias)]
+    anywhere = pl.BlockSpec(memory_space=pl.ANY)
+    vmem = pl.BlockSpec(memory_space=pltpu.VMEM)
+    half = HD // 2
+    copies = 256
+    scratch = [
+        ((4, 2, nz, NY, rows, width), BF16),
+        ((2, nz, NY, rows, width), BF16),
+        ((4, nz // 2, rows, width), BF16),
+        ((4, nz - nz // 2, rows, width), BF16),
+        ((4, nz, rows, width), BF16),
+        ((4, nz, rows, width), BF16),
+        ((4, nz, rows, width), BF16),
+        ((4, quarter, width), BF16),
+        ((width, length), BF16),
+        ((width, length), BF16),
+        ((width, length), BF16),
+        ((2, quarter, width), BF16),
+        ((length, LANES), F32),
+        ((length, LANES), F32),
+        ((length, LANES), F32),
+        ((half, length), F32),
+        ((half, length), F32),
+        ((2, 5, length, LANES), BF16),
+        ((6, LANES, length), BF16),
+        ((6, HD, length), BF16),
+        ((6, HD, length), BF16),
+        ((6, 1, length), F32),
+        ((6, 1, length), F32),
+        ((2, length, 2 * LANES), BF16),
+        ((6, HD, length), BF16),
+        ((2, quarter, width), F32),
+        ((2, quarter, LANES), F32),
+        ((4, quarter, width), BF16),
+        ((2, length, width), BF16),
+        ((2, length, width), BF16),
+        ((2, length, width), BF16),
+        ((2, quarter, width), F32),
+        ((2, quarter, width), BF16),
+        ((2, 2, quarter, width), BF16),
+        ((2, quarter, width), F32),
+        ((2, 2, quarter, width), BF16),
+        ((length, LANES), F32),
+        ((length, LANES), F32),
+        ((8, width), F32),
+        ((3, 8, width), F32),
+        ((3, 8, width), F32),
+        ((nz, 8, width), F32),
+    ]
+    outputs, grad_input, grads, norms = pl.pallas_call(
+        functools.partial(layer_kernel, nz),
+        out_shape=(
+            jax.ShapeDtypeStruct(layer_input.shape, BF16),
+            jax.ShapeDtypeStruct(layer_input.shape, BF16),
+            jax.ShapeDtypeStruct((4, rows, width), F32),
+            jax.ShapeDtypeStruct((8, width), F32),
+        ),
+        in_specs=[anywhere, anywhere, vmem, anywhere] + [vmem] * 4 + [anywhere] * 4,
+        out_specs=(anywhere, anywhere, anywhere, vmem),
+        scratch_shapes=[pltpu.VMEM(shape, kind) for shape, kind in scratch]
+        + [
+            pltpu.SemaphoreType.DMA((16,)),
+            pltpu.SemaphoreType.DMA((copies,)),
+            pltpu.SemaphoreType.DMA((copies,)),
+        ],
+        compiler_params=pltpu.CompilerParams(
+            collective_id=0, has_side_effects=True, vmem_limit_bytes=VMEM_BYTES
+        ),
+    )(layer_input, cotangent, segment_ids, packed, *vectors, *tables)
+    attention, gate, up, down = grads
+    b = [attention[:, i * LANES : (i + 1) * LANES] for i in range(6)]
+    grad_query = jnp.concatenate([b[0], b[3][:, :HD]], axis=1)
+    grad_key = jnp.concatenate([b[1], b[3][:, HD:]], axis=1)
+    grad_value = jnp.concatenate([b[2], b[4][:, :HD]], axis=1)
+    grad_output = jnp.concatenate([b[5], b[4][:, HD:]], axis=1).T
+    return (
+        outputs,
+        grad_input,
+        grad_query,
+        grad_key,
+        grad_value,
+        grad_output,
+        gate,
+        up,
+        down.T,
+        norms[0],
+        norms[1],
+        norms[2],
+        norms[3],
+    )
+
+
+VMEM_BYTES = 64 << 20
 
 
 def solution(mesh):
@@ -350,6 +1185,24 @@
         P(),
         P(),
     )
-    return jax.shard_map(
-        per_device, mesh=mesh, in_specs=in_specs, out_specs=out_specs, check_vma=False
-    )
+    dp_size, tensor_size = mesh.shape["dp"], mesh.shape["tensor"]
+
+    def whole(*arrays):
+        layer_input, query_weight, gate_weight = arrays[0], arrays[3], arrays[7]
+        batch, length, width = layer_input.shape
+        fits = (
+            tensor_size == 4
+            and dp_size % (2 * NY) == 0
+            and batch == 2 * dp_size
+            and width % (16 * dp_size) == 0
+            and query_weight.shape[1] == 12 * HD
+            and query_weight.shape[1] == width
+            and gate_weight.shape[1] == 4 * width
+            and length % 1024 == 0
+        )
+        program = functools.partial(layer_per_device, dp_size) if fits else per_device
+        return jax.shard_map(
+            program, mesh=mesh, in_specs=in_specs, out_specs=out_specs, check_vma=False
+        )(*arrays)
+
+    return whole

time: 1520 us -> 276 us (0.18)
  waiting for transfers between devices: 899 us -> 0 us
  blocking collectives: 292 us -> 0 us
  Pallas kernels: 0 us -> 253 us
  matrix products: 147 us -> 0 us
  other arithmetic: 72.1 us -> 3.29 us
  local copies, waits for them, and re-layouts: 78.3 us -> 16.8 us
  between operations: 16.1 us -> 0.7 us
    reduce_scatter x14 -> x0, waiting for transfers between devices: 600 us -> none  [the longest x5 340 us: per_device(): lax.psum_scatter(row_grads, 'dp', scatter_dimension=0, tiled=True)]
    all_gather x14 -> x0, waiting for transfers between devices: 279 us -> none  [the longest x2 78.1 us: fetch_weights(): lax.all_gather(up_weight, 'dp', axis=0, tiled=True)]
    pallas_call x0 -> x1, Pallas kernels: none -> 253 us  [layer_per_device(): pl.pallas_call(functools.partial(layer_kernel, nz), out_shape=(jax.ShapeD...]
    all_gather x8 -> x0, blocking collectives: 252 us -> none  [the longest x2 64.6 us: fetch_weights(): lax.all_gather(output_weight, 'dp', axis=1, tiled=True)]
    dot_general x70 -> x0, matrix products: 147 us -> none  [the longest x14 30 us: times_transpose(): lax.dot_general(left, right, (((1,), (1,)), ((), ())), preferred_element_...]
    psum x1 -> x0, blocking collectives: 39.7 us -> none  [per_device(): norm_done = lax.psum(norm_parts, ('dp', 'tensor'))]
    dynamic_update_slice x8 -> x0, local copies, waits for them, and re-layouts: 33.9 us -> none  [micro_step(): lax.map(attend_forward, (query_blocks, segment_blocks))]
    reduce_sum x22 -> x0, other arithmetic: 31.7 us -> none  [the longest x6 10.5 us: layer_norm(): return centred * lax.rsqrt(variance + eps_norm) * gain_vec + bias_vec]
  transfers between devices with their start and end apart: 29 -> 0, of which waited for: 27 -> 0; matrix products, arithmetic and copies ran while one was open for 5% -> 0% of each run, Pallas kernels for 0% -> 0%
where the time goes in v1:
time: 276 us; the launch traced here: 274 us
  Pallas kernels  253 us (92%)
  local copies, waits for them, and re-layouts  16.8 us (6%)
  other arithmetic  3.29 us (1%)
    pallas_call x1, Pallas kernels, layer_per_device(): pl.pallas_call(functools.partial(layer_kernel, nz), out_shape=(jax.ShapeD...  253 us

profile of v1, /device:TPU:0, one launch (start us, length us, event | category | flops | bytes accessed | tf_op | source)
XLA Modules:
  0.0 274.1 jit_solution(11122040252333096163)
XLA Ops:
  0.6 1.3 reshape.38.g1_ref
  1.9 1.3 reshape.39.b1_ref
  3.2 1.3 reshape.40.g2_ref
  4.4 1.3 reshape.41.b2_ref
  5.7 0.7 slice.69
  6.5 0.7 slice.66
  7.2 0.7 slice.70
  7.9 0.7 slice.67
  8.7 0.7 slice.71
  9.4 0.7 slice.68
  10.1 0.9 copy.31
  11.1 0.1 concatenate.15
  11.2 1.9 pad_maximum_fusion.wpk
  13.1 253.4 %shard_map.273 = (bf16[2,256,768]{2,1,0:T(8,128)(2,1)}, bf16[2,256,768]{2,1,0:T(8,128)(2,1)}, f32[4,96,768]{2,1,0:T(8,128)}, f32[8,768]{1,0:T(8,128)}) custom-call(bf16[2,256,768]{2,1,0:T(8,128)(2,1)} %xin.1, bf16[2,256,768]{2,1,0:T(8,128)(2,1)} %cot.1, s32[2,1024]{1,0:T(2,128)} %seg.1, bf16[4,96,768]{2,1,0:T(8,128)(2,1)} %pad_maximum_fusion.wpk, ...), custom_call_target="tpu_custom_call" | custom-call | tf_op jit(solution)/shard_map/pallas_call | solution.py:1110
  266.5 1.5 slice_reduce_fusion
  268.0 2.2 slice_bitcast_fusion
  270.2 0.0 copy-start.1
  270.2 0.1 fusion.1
  270.3 0.7 pad_maximum_fusion.3
  270.9 0.0 copy-start
  270.9 0.7 copy.32
  271.7 0.7 pad_maximum_fusion.1
  272.4 0.0 copy-done.1
  272.4 0.9 copy.35
  273.2 0.0 copy-done
  273.3 0.9 copy.36
  (3 shorter events, 0.0 us)
Async XLA Ops:
  270.2 2.2 copy-start.1
  270.9 2.3 copy-start

commit v2 on v1

--- a/solution.py
+++ b/solution.py
@@ -371,12 +371,18 @@
     nz,
     xin,
     cot,
-    seg,
-    wpk,
-    g1_ref,
-    b1_ref,
-    g2_ref,
-    b2_ref,
+    seg_h,
+    wq_h,
+    wk_h,
+    wv_h,
+    wo_h,
+    wg_h,
+    wu_h,
+    wd_h,
+    g1_h,
+    b1_h,
+    g2_h,
+    b2_h,
     cosl_h,
     sinl_h,
     cosf_h,
@@ -423,10 +429,17 @@
     OB,
     DKA,
     DVA,
+    SEG,
+    WQ,
+    WK,
+    WV,
+    WO,
+    VEC,
     NG,
     NR,
     NS,
     NZR,
+    ZB,
     loc,
     ssem,
     rsem,
@@ -479,7 +492,10 @@
         copy.start()
         return copy
 
-    l_w = lc(wpk, W.at[:, 0, z, y])
+    l_out, l_att = lc(wo_h, WO), [lc(wq_h, WQ), lc(wk_h, WK), lc(wv_h, WV)]
+    l_w = [lc(wg_h, W.at[1, 0, z, y]), lc(wu_h, W.at[2, 0, z, y]), lc(wd_h, W.at[3, 0, z, y])]
+    l_seg = lc(seg_h, SEG)
+    l_vec = [lc(h, VEC.at[i, 0]) for i, h in enumerate((g1_h, b1_h, g2_h, b2_h))]
     l_x = lc(xin.at[xi], X.at[tt])
     l_ct = lc(cot.at[xi], CT.at[xi])
     l_tab = [lc(cosl_h, COSL), lc(sinl_h, SINL), lc(cosf_h, COSF), lc(sinf_h, SINF)]
@@ -488,46 +504,100 @@
     peers = [dev_x, dev_c, dev_y] + dev_z[1:]
     for dev in peers:
         pl.semaphore_signal(barrier, inc=1, device_id=dev, device_id_type=MESH)
+    l_out.wait()
+    for copy in l_att:
+        copy.wait()
+    shards = [W.at[0, 0, z, y], wg_h, wu_h, wd_h]
+    two = 2 * HD
+    turned_out = WO[...].T
+    shards[0][:, :two] = WQ[:, :two]
+    shards[0][:, two : 2 * two] = WK[:, :two]
+    shards[0][:, 2 * two : 3 * two] = WV[:, :two]
+    shards[0][:, 3 * two : 4 * two] = jnp.concatenate([WQ[:, two:], WK[:, two:]], axis=1)
+    shards[0][:, 4 * two : 5 * two] = jnp.concatenate([WV[:, two:], turned_out[:, two:]], axis=1)
+    shards[0][:, 5 * two :] = turned_out[:, :two]
     pl.semaphore_wait(barrier, len(peers))
 
     ag = {}
-
-    def e1(k):
-        own = wpk.at[k]
-        ag[k, "z"] = [rc(own, W.at[k, 0, z, y], dev_z[j]) for j in range(1, nz)]
-        ag[k, "x"] = [rc(own, W.at[k, 1, z, y], dev_x)]
-        ag[k, "y"] = [rc(own, W.at[k, 0, z, y], dev_y)]
-
-    def e2(k):
+    half_cols = width // 2
+    pieces = [(0, 0, width), (1, 0, width), (2, 0, width), (3, 0, half_cols), (3, half_cols, half_cols)]
+    LAST = 4
+
+    def cut(view, p):
+        _, lo, n = pieces[p]
+        return view if n == width else view.at[..., pl.ds(lo, n)]
+
+    def w_at(p, s, zz, yy):
+        return cut(W.at[pieces[p][0], s, zz, yy], p)
+
+    def own_shard(p):
+        return cut(shards[pieces[p][0]], p)
+
+    def e1_plane(p):
+        own = own_shard(p)
+        ag[p, "x"] = [rc(own, w_at(p, 1, z, y), dev_x)]
+        ag[p, "y"] = [rc(own, w_at(p, 0, z, y), dev_y)]
+
+    def e1(p):
+        own = own_shard(p)
+        ag[p, "z"] = [rc(own, w_at(p, 0, z, y), dev_z[j]) for j in range(1, nz)]
+        e1_plane(p)
+
+    def e2(p):
         for j in range(1, nz):
-            ag[k, "z"][j - 1].wait_recv()
-            part = W.at[k, 0, zfrom[j], y]
-            ag[k, "x"].append(rc(part, W.at[k, 1, zfrom[j], y], dev_x))
-            ag[k, "y"].append(rc(part, part, dev_y))
-
-    def e3(k):
-        ag[k, "d"] = []
+            ag[p, "z"][j - 1].wait_recv()
+            part = w_at(p, 0, zfrom[j], y)
+            ag[p, "x"].append(rc(part, w_at(p, 1, zfrom[j], y), dev_x))
+            ag[p, "y"].append(rc(part, part, dev_y))
+
+    def e3(p, by_x):
+        ag[p, "d"] = []
         for j in range(nz):
-            ag[k, "x"][j].wait_recv()
-            if j < hz:
-                part = W.at[k, 1, zfrom[j], y]
-                ag[k, "d"].append(rc(part, part, dev_y))
-            ag[k, "y"][j].wait_recv()
-            if j >= hz:
-                ag[k, "d"].append(rc(W.at[k, 0, zfrom[j], oy], W.at[k, 1, zfrom[j], oy], dev_x))
-
-    def e4(k):
-        for copy in ag[k, "d"]:
+            ag[p, "x"][j].wait_recv()
+            if j < nz - by_x:
+                part = w_at(p, 1, zfrom[j], y)
+                ag[p, "d"].append(rc(part, part, dev_y))
+            ag[p, "y"][j].wait_recv()
+            if j >= nz - by_x:
+                ag[p, "d"].append(rc(w_at(p, 0, zfrom[j], oy), w_at(p, 1, zfrom[j], oy), dev_x))
+
+    def e4(p):
+        for copy in ag[p, "d"]:
             copy.wait_recv()
 
-    def e_sent(k):
-        for copy in ag[k, "z"] + ag[k, "x"] + ag[k, "y"] + ag[k, "d"]:
+    top_rows, low_rows = pl.ds(0, rows // 2), pl.ds(rows // 2, rows // 2)
+
+    def f2(p):
+        ag[p, "x"][0].wait_recv()
+        part = w_at(p, 1, z, y).at[top_rows]
+        ag[p, "d"] = [rc(part, part, dev_y)]
+        ag[p, "y"][0].wait_recv()
+        ag[p, "d"].append(
+            rc(w_at(p, 0, z, oy).at[low_rows], w_at(p, 1, z, oy).at[low_rows], dev_x)
+        )
+
+    def f3(p):
+        for copy in ag[p, "d"]:
+            copy.wait_recv()
+        plane = cut(W.at[3, :, z], p)
+        ag[p, "z"] = [rc(plane, plane, dev_z[j]) for j in range(1, nz)]
+
+    def f4(p):
+        for copy in ag[p, "z"]:
+            copy.wait_recv()
+
+    def e_sent(p):
+        for copy in ag[p, "z"] + ag[p, "x"] + ag[p, "y"] + ag[p, "d"]:
             sent(copy)
 
     x_far = rc(xin.at[1 - xi], X.at[tt], dev_x)
     x_core = rc(xin.at[xi], X.at[tt], dev_c)
     e1(0)
-
+    e1_plane(LAST)
+
+    l_seg.wait()
+    seg = SEG
+    g1_ref, b1_ref, g2_ref, b2_ref = (VEC.at[i] for i in range(4))
     SC[...] = jnp.broadcast_to(seg[pl.ds(xi, 1), :].astype(F32), (LANES, length)).T
     NG[...] = jnp.zeros_like(NG)
     lane = lax.broadcasted_iota(jnp.int32, (1, LANES), 1)
@@ -555,17 +625,15 @@
     x_core2 = rc(X.at[t_x], X.at[t_x], dev_c)
     x_core.wait_recv()
     l_x.wait()
-    l_w.wait()
     l_ct.wait()
-    for copy in l_tab:
+    for copy in l_w + l_vec + l_tab:
         copy.wait()
     x_core2.wait_recv()
     turn_rows(X, XT)
     e2(0)
     e1(1)
-    ct_far = rc(cot.at[1 - xi], CT.at[xi], dev_x)
-    e3(0)
-    e4(0)
+    f2(LAST)
+    e3(0, 1)
 
     def project(s):
         def step(i, _):
@@ -605,10 +673,10 @@
         query_seg = seg[pl.ds(xi, 1), at].astype(F32)
         return jnp.where(key_seg == query_seg, st, mask_fill)
 
-    def attend(s):
+    def attend(first, heads):
         def step(n, _):
-            hh = lax.div(n, 4)
-            h = 3 * s + hh
+            h = first + lax.div(n, 4)
+            s, hh = lax.div(h, 3), lax.rem(h, 3)
             at = at_quarter(lax.rem(n, 4))
             st = scores_of(s, hh, h, at)
             top = jnp.max(st, axis=0, keepdims=True)
@@ -619,8 +687,9 @@
             ATTT[h, :, at] = ot.astype(BF16)
             return 0
 
-        lax.fori_loop(0, 12, step, 0)
-
+        lax.fori_loop(0, 4 * heads, step, 0)
+
+    def turn_heads(s):
         def turn(i, _):
             at = at_quarter(i)
             pair = jnp.concatenate([ATTT[3 * s, :, at], ATTT[3 * s + 1, :, at]], axis=0)
@@ -632,15 +701,21 @@
         lax.fori_loop(0, 4, turn, 0)
 
     project(0)
-    project(1)
     e2(1)
     e1(2)
-    attend(0)
-    e3(1)
+    e4(0)
+    project(1)
+    attend(0, 2)
+    e3(1, 2)
     e2(2)
     e1(3)
-    attend(1)
-
+    attend(2, 2)
+    ct_far = rc(cot.at[1 - xi], CT.at[xi], dev_x)
+    f3(LAST)
+    attend(4, 2)
+    e4(1)
+    turn_heads(0)
+    turn_heads(1)
     last_exchange = []
 
     def exchange(n, part):
@@ -689,17 +764,13 @@
 
     over_tiles(first_norm)
     h_copies = spread()
-    e4(1)
+    e3(2, 1)
     for copy in h_copies:
         copy.wait_recv()
     turn_rows(F4, TT)
-    e3(2)
     e2(3)
-    e4(2)
-
-    def ff_up(n, _):
-        s = lax.div(n, 4)
-        i = lax.rem(n, 4)
+
+    def ff_up(s, i):
         at = at_quarter(i)
         g = mm(F4[i], wmat(1, s))
         u = mm(F4[i], wmat(2, s))
@@ -708,9 +779,12 @@
         RR[s, at, :] = (g * jax.nn.sigmoid(g) * u).astype(BF16)
         return 0
 
-    lax.fori_loop(0, 8, ff_up, 0)
-    e3(3)
+    lax.fori_loop(0, 4, lambda i, _: ff_up(0, i), 0)
+    e4(2)
+    e3(3, 1)
+    lax.fori_loop(0, 4, lambda i, _: ff_up(1, i), 0)
     e4(3)
+    f4(LAST)
 
     def down_part(i):
         at = at_quarter(i)
@@ -740,65 +814,122 @@
 
     slots = {3: G, 1: W.at[3], 2: W.at[1], 0: W.at[2]}
     rs = {}
-    lo_z, hi_z = pl.ds(0, hz), pl.ds(hz, nz - hz)
-
-    def r1(k):
-        g = slots[k]
-        rs[k, "dx"] = rc(g.at[1, lo_z, oy], S1X.at[k], dev_x)
-        rs[k, "dy"] = rc(g.at[1, hi_z, oy], S1Y.at[k], dev_y)
-        rs[k, "x0"] = rc(g.at[1, lo_z, y], S2X.at[k, lo_z], dev_x)
-        rs[k, "y0"] = rc(g.at[0, hi_z, oy], S2Y.at[k, hi_z], dev_y)
-
-    def r2(k):
-        g = slots[k]
-        rs[k, "dx"].wait_recv()
-        for j in range(hz):
-            g[0, j, oy] = (g[0, j, oy].astype(F32) + S1X[k, j].astype(F32)).astype(BF16)
-        rs[k, "y1"] = rc(g.at[0, lo_z, oy], S2Y.at[k, lo_z], dev_y)
-        rs[k, "dy"].wait_recv()
-        for j in range(hz, nz):
-            g[1, j, y] = (g[1, j, y].astype(F32) + S1Y[k, j - hz].astype(F32)).astype(BF16)
-        rs[k, "x1"] = rc(g.at[1, hi_z, y], S2X.at[k, hi_z], dev_x)
-
-    def r3(k):
-        g = slots[k]
+    by_x = {0: 1, 1: 1, 2: 1, 3: 2}
+
+    def g_at(p, s, zz, yy):
+        return cut(slots[pieces[p][0]].at[s, zz, yy], p)
+
+    def into(ref, p, *at):
+        return cut(ref.at[(pieces[p][0],) + at], p)
+
+    def plus(target, *others):
+        total = target[...].astype(F32)
+        for other in others:
+            total = total + other[...].astype(F32)
+        target[...] = total.astype(BF16)
+
+    def early(p):
+        return pl.ds(0, by_x[p]), pl.ds(by_x[p], nz - by_x[p])
+
+    def r1_far(p):
+        nx = by_x[p]
+        near, far = early(p)
+        rs[p, "dx"] = rc(g_at(p, 1, near, oy), into(S1X, p, pl.ds(0, nx)), dev_x)
+        rs[p, "dy"] = rc(g_at(p, 1, far, oy), into(S1Y, p, pl.ds(0, nz - nx)), dev_y)
+        rs[p, "x0"] = rc(g_at(p, 1, near, y), into(S2X, p, near), dev_x)
+
+    def r1_near(p):
+        _, far = early(p)
+        rs[p, "y0"] = rc(g_at(p, 0, far, oy), into(S2Y, p, far), dev_y)
+
+    def r2(p):
+        nx = by_x[p]
+        near, far = early(p)
+        rs[p, "dx"].wait_recv()
+        for j in range(nx):
+            plus(g_at(p, 0, j, oy), into(S1X, p, j))
+        rs[p, "y1"] = rc(g_at(p, 0, near, oy), into(S2Y, p, near), dev_y)
+        rs[p, "dy"].wait_recv()
+        for j in range(nx, nz):
+            plus(g_at(p, 1, j, y), into(S1Y, p, j - nx))
+        rs[p, "x1"] = rc(g_at(p, 1, far, y), into(S2X, p, far), dev_x)
+
+    def r3(p):
         for name in ("x0", "y0", "y1", "x1"):
-            rs[k, name].wait_recv()
+            rs[p, name].wait_recv()
         for j in range(nz):
-            g[0, j, y] = (
-                g[0, j, y].astype(F32) + S2X[k, j].astype(F32) + S2Y[k, j].astype(F32)
-            ).astype(BF16)
-        rs[k, "z"] = [rc(g.at[0, zs[j], y], ZR.at[k, z], dev_z[j]) for j in range(1, nz)]
-
-    def r4(k):
-        g = slots[k]
-        for copy in rs[k, "z"]:
+            plus(g_at(p, 0, j, y), into(S2X, p, j), into(S2Y, p, j))
+        rs[p, "z"] = [rc(g_at(p, 0, zs[j], y), into(ZR, p, z), dev_z[j]) for j in range(1, nz)]
+
+    def place(p):
+        k = pieces[p][0]
+        return cut(N1.at[k // 2, pl.ds((k % 2) * rows, rows)], p)
+
+    def r4(p):
+        for copy in rs[p, "z"]:
             copy.wait_recv()
-        total = g[0, z, y].astype(F32)
+        total = g_at(p, 0, z, y)[...].astype(F32)
         for j in range(1, nz):
-            total = total + ZR[k, zfrom[j]].astype(F32)
-        place = N1.at[k // 2, pl.ds((k % 2) * rows, rows)]
-        place[...] = total
-        rs[k, "out"] = lc(place, gw_h.at[k])
-
-    def weight_grad(k, left, right):
-        g = slots[k]
+            total = total + into(ZR, p, zfrom[j])[...].astype(F32)
+        target = place(p)
+        target[...] = total
+        rs[p, "out"] = lc(target, cut(gw_h.at[pieces[p][0]], p))
+
+    def q1(p):
+        rs[p, "z"] = [
+            rc(cut(slots[3].at[:, zs[j]], p), ZB.at[z], dev_z[j]) for j in range(1, nz)
+        ]
+
+    def q2(p):
+        for copy in rs[p, "z"]:
+            copy.wait_recv()
+        for s in range(2):
+            for yy in range(NY):
+                plus(g_at(p, s, z, yy), *(ZB.at[zfrom[j], s, yy] for j in range(1, nz)))
+        rs[p, "dx"] = rc(g_at(p, 1, z, oy).at[top_rows], into(S1X, p, 0).at[top_rows], dev_x)
+        rs[p, "dy"] = rc(g_at(p, 1, z, oy).at[low_rows], into(S1Y, p, 0).at[low_rows], dev_y)
+        rs[p, "x0"] = rc(g_at(p, 1, z, y).at[top_rows], into(S2X, p, 0).at[top_rows], dev_x)
+        rs[p, "y0"] = rc(g_at(p, 0, z, oy).at[low_rows], into(S2Y, p, 0).at[low_rows], dev_y)
+
+    def q3(p):
+        rs[p, "dx"].wait_recv()
+        plus(g_at(p, 0, z, oy).at[top_rows], into(S1X, p, 0).at[top_rows])
+        rs[p, "y1"] = rc(g_at(p, 0, z, oy).at[top_rows], into(S2Y, p, 0).at[top_rows], dev_y)
+        rs[p, "dy"].wait_recv()
+        plus(g_at(p, 1, z, y).at[low_rows], into(S1Y, p, 0).at[low_rows])
+        rs[p, "x1"] = rc(g_at(p, 1, z, y).at[low_rows], into(S2X, p, 0).at[low_rows], dev_x)
+
+    def q4(p):
+        for name in ("x0", "y0", "y1", "x1"):
+            rs[p, name].wait_recv()
+        total = g_at(p, 0, z, y)[...].astype(F32)
+        total = total + into(S2X, p, 0)[...].astype(F32) + into(S2Y, p, 0)[...].astype(F32)
+        target = place(p)
+        target[...] = total
+        rs[p, "out"] = lc(target, cut(gw_h.at[3], p))
+
+    def weight_grad(p, s, left, right):
+        k, lo, n = pieces[p]
         block = NY * rows
 
-        def step(n, _):
-            s = lax.div(n, nz)
-            j = lax.rem(n, nz)
+        def step(j, _):
             at = pl.ds(pl.multiple_of(j * block, block), block)
-            g[s, j] = mm(left[at, :], right[s]).astype(BF16).reshape(NY, rows, width)
+            part = mm(left[at, :], right[s, :, lo : lo + n]).astype(BF16)
+            slots[k][s, j, :, :, lo : lo + n] = part.reshape(NY, rows, n)
             return 0
 
-        lax.fori_loop(0, 2 * nz, step, 0)
+        lax.fori_loop(0, nz, step, 0)
 
     for copy in d_copies:
         copy.wait_recv()
     turn_rows(F4, DT)
-    weight_grad(3, DT, RR)
-    r1(3)
+    weight_grad(LAST, 0, DT, RR)
+    weight_grad(LAST, 1, DT, RR)
+    q1(LAST)
+    weight_grad(3, 1, DT, RR)
+    r1_far(3)
+    weight_grad(3, 0, DT, RR)
+    r1_near(3)
 
     def ff_back(n, _):
         s = lax.div(n, 4)
@@ -813,10 +944,13 @@
         return 0
 
     lax.fori_loop(0, 8, ff_back, 0)
+    r2(3)
     e_sent(3)
-    weight_grad(1, TT, GP)
-    r1(1)
-    r2(3)
+    e_sent(LAST)
+    weight_grad(1, 1, TT, GP)
+    r1_far(1)
+    weight_grad(1, 0, TT, GP)
+    r1_near(1)
 
     def hidden_part(i):
         at = at_quarter(i)
@@ -845,9 +979,11 @@
     n_core = rc(NG, NR.at[0], dev_c)
     e_sent(1)
     e_sent(2)
-    weight_grad(2, TT, UP)
+    weight_grad(2, 1, TT, UP)
+    r1_far(2)
+    weight_grad(2, 0, TT, UP)
+    r1_near(2)
     r3(3)
-    r1(2)
     r2(1)
     for copy in b_copies:
         copy.wait_recv()
@@ -896,10 +1032,9 @@
     n_x.wait_recv()
     NS[1] = NS[0] + NR[1]
     n_y = rc(NS.at[1], NR.at[2], dev_y)
-    r2(2)
-    r3(1)
-
-    def attend_back(s):
+    q2(LAST)
+
+    def attend_back(s, first, heads):
         def head(hh, _):
             h = 3 * s + hh
             DKA[...] = jnp.zeros_like(DKA)
@@ -932,8 +1067,9 @@
             lax.fori_loop(0, 4, finish, 0)
             return 0
 
-        lax.fori_loop(0, 3, head, 0)
-
+        lax.fori_loop(first, first + heads, head, 0)
+
+    def join_heads(s):
         def gather(i, _):
             at = at_quarter(i)
 
@@ -958,31 +1094,43 @@
 
         lax.fori_loop(0, 4, gather, 0)
 
-    attend_back(0)
+    def in_grad(s):
+        block = NY * rows
+
+        def step(j, _):
+            at = pl.ds(pl.multiple_of(j * block, block), block)
+            part = mm(XT[at, :], RR[s, :, : 5 * LANES])
+            mixed = slots[0][s, j, :, :, 4 * LANES : 5 * LANES].reshape(block, LANES)
+            mixed = (part[:, 4 * LANES :] + mixed.astype(F32)).astype(BF16)
+            slots[0][s, j, :, :, : 4 * LANES] = (
+                part[:, : 4 * LANES].astype(BF16).reshape(NY, rows, 4 * LANES)
+            )
+            slots[0][s, j, :, :, 4 * LANES : 5 * LANES] = mixed.reshape(NY, rows, LANES)
+            return 0
+
+        lax.fori_loop(0, nz, step, 0)
+
+    attend_back(1, 0, 1)
+    r2(2)
+    r3(1)
+    attend_back(1, 1, 2)
+    q3(LAST)
     r4(3)
-    r3(2)
+    join_heads(1)
+    in_grad(1)
+    r1_far(0)
     n_y.wait_recv()
     NS[2] = NS[1] + NR[2]
     NZR[z] = NS[2]
     n_z = [rc(NS.at[2], NZR.at[z], dev_z[j]) for j in range(1, nz)]
-    attend_back(1)
-
-    def in_grad(n, _):
-        s = lax.div(n, nz)
-        j = lax.rem(n, nz)
-        block = NY * rows
-        at = pl.ds(pl.multiple_of(j * block, block), block)
-        part = mm(XT[at, :], RR[s, :, : 5 * LANES])
-        mixed = slots[0][s, j, :, :, 4 * LANES : 5 * LANES].reshape(block, LANES)
-        mixed = (part[:, 4 * LANES :] + mixed.astype(F32)).astype(BF16)
-        slots[0][s, j, :, :, : 4 * LANES] = (
-            part[:, : 4 * LANES].astype(BF16).reshape(NY, rows, 4 * LANES)
-        )
-        slots[0][s, j, :, :, 4 * LANES : 5 * LANES] = mixed.reshape(NY, rows, LANES)
-        return 0
-
-    lax.fori_loop(0, 2 * nz, in_grad, 0)
-    r1(0)
+    attend_back(0, 0, 2)
+    r3(2)
+    q4(LAST)
+    attend_back(0, 2, 1)
+    join_heads(0)
+    in_grad(0)
+    r1_near(0)
+    r2(0)
     r4(1)
 
     def input_part(i):
@@ -1000,7 +1148,6 @@
     over_tiles(input_grad)
     i_far = rc(OB.at[1, 1 - xi], gin_h.at[xi], dev_x)
     i_own = lc(OB.at[1, xi], gin_h.at[xi])
-    r2(0)
     r4(2)
     for copy in n_z:
         copy.wait_recv()
@@ -1014,8 +1161,8 @@
     i_far.wait_recv()
     o_own.wait()
     i_own.wait()
-    for k in range(4):
-        rs[k, "out"].wait()
+    for p in range(5):
+        rs[p, "out"].wait()
     for copy in list(sends.values()):
         sent(copy)
 
@@ -1041,33 +1188,17 @@
     length = 4 * quarter
     rows = query_weight.shape[0]
     nz = dp_size // NY
-    out_turned = output_weight.T
-    two = 2 * HD
-    attention_pack = jnp.concatenate(
-        [
-            query_weight[:, :two],
-            key_weight[:, :two],
-            value_weight[:, :two],
-            query_weight[:, two:],
-            key_weight[:, two:],
-            value_weight[:, two:],
-            out_turned[:, two:],
-            out_turned[:, :two],
-        ],
-        axis=1,
-    )
-    packed = jnp.stack([attention_pack, gate_weight, up_weight, down_weight.T])
     tables = [jnp.asarray(t) for t in lane_tables(length)]
-    vectors = [v.reshape(1, width) for v in (first_gain, first_bias, second_gain, second_bias)]
     anywhere = pl.BlockSpec(memory_space=pl.ANY)
     vmem = pl.BlockSpec(memory_space=pltpu.VMEM)
     half = HD // 2
-    copies = 256
+    copies = 134
+    part = query_weight.shape[1]
     scratch = [
         ((4, 2, nz, NY, rows, width), BF16),
         ((2, nz, NY, rows, width), BF16),
         ((4, nz // 2, rows, width), BF16),
-        ((4, nz - nz // 2, rows, width), BF16),
+        ((4, nz - 1, rows, width), BF16),
         ((4, nz, rows, width), BF16),
         ((4, nz, rows, width), BF16),
         ((4, nz, rows, width), BF16),
@@ -1102,10 +1233,17 @@
         ((2, 2, quarter, width), BF16),
         ((length, LANES), F32),
         ((length, LANES), F32),
+        ((2, length), jnp.int32),
+        ((rows, part), BF16),
+        ((rows, part), BF16),
+        ((rows, part), BF16),
+        ((part, rows), BF16),
+        ((4, 1, width), F32),
         ((8, width), F32),
         ((3, 8, width), F32),
         ((3, 8, width), F32),
         ((nz, 8, width), F32),
+        ((nz, 2, NY, rows, width // 2), BF16),
     ]
     outputs, grad_input, grads, norms = pl.pallas_call(
         functools.partial(layer_kernel, nz),
@@ -1115,39 +1253,130 @@
             jax.ShapeDtypeStruct((4, rows, width), F32),
             jax.ShapeDtypeStruct((8, width), F32),
         ),
-        in_specs=[anywhere, anywhere, vmem, anywhere] + [vmem] * 4 + [anywhere] * 4,
+        in_specs=[anywhere] * 18,
         out_specs=(anywhere, anywhere, anywhere, vmem),
         scratch_shapes=[pltpu.VMEM(shape, kind) for shape, kind in scratch]
         + [
-            pltpu.SemaphoreType.DMA((16,)),
+            pltpu.SemaphoreType.DMA((25,)),
             pltpu.SemaphoreType.DMA((copies,)),
             pltpu.SemaphoreType.DMA((copies,)),
         ],
         compiler_params=pltpu.CompilerParams(
             collective_id=0, has_side_effects=True, vmem_limit_bytes=VMEM_BYTES
         ),
-    )(layer_input, cotangent, segment_ids, packed, *vectors, *tables)
-    attention, gate, up, down = grads
-    b = [attention[:, i * LANES : (i + 1) * LANES] for i in range(6)]
-    grad_query = jnp.concatenate([b[0], b[3][:, :HD]], axis=1)
-    grad_key = jnp.concatenate([b[1], b[3][:, HD:]], axis=1)
-    grad_value = jnp.concatenate([b[2], b[4][:, :HD]], axis=1)
-    grad_output = jnp.concatenate([b[5], b[4][:, HD:]], axis=1).T
-    return (
-        outputs,
-        grad_input,
-        grad_query,
-        grad_key,
-        grad_value,
-        grad_output,
-        gate,
-        up,
-        down.T,
-        norms[0],
-        norms[1],
-        norms[2],
-        norms[3],
+    )(
+        layer_input,
+        cotangent,
+        segment_ids,
+        query_weight,
+        key_weight,
+        value_weight,
+        output_weight,
+        gate_weight,
+        up_weight,
+        down_weight.T,
+        first_gain,
+        first_bias,
+        second_gain,
+        second_bias,
+        *tables,
     )
+    vector = jax.ShapeDtypeStruct((width,), F32)
+    like = lambda a: jax.ShapeDtypeStruct(a.shape, F32)
+    results = pl.pallas_call(
+        place_kernel,
+        out_shape=(
+            jax.ShapeDtypeStruct(layer_input.shape, BF16),
+            jax.ShapeDtypeStruct(layer_input.shape, BF16),
+            like(query_weight),
+            like(key_weight),
+            like(value_weight),
+            like(output_weight),
+            like(gate_weight),
+            like(up_weight),
+            jax.ShapeDtypeStruct(down_weight.shape[::-1], F32),
+            vector,
+            vector,
+            vector,
+            vector,
+        ),
+        in_specs=[anywhere] * 4,
+        out_specs=(anywhere, anywhere) + (vmem,) * 4 + (anywhere,) * 3 + (vmem,) * 4,
+        scratch_shapes=[
+            pltpu.VMEM(layer_input.shape, BF16),
+            pltpu.VMEM(layer_input.shape, BF16),
+            pltpu.VMEM((4, rows, width), F32),
+            pltpu.VMEM((8, width), F32),
+            pltpu.SemaphoreType.DMA((7,)),
+            pltpu.SemaphoreType.DMA((5,)),
+        ],
+        compiler_params=pltpu.CompilerParams(vmem_limit_bytes=VMEM_BYTES),
+    )(outputs, grad_input, grads, norms)
+    return (*results[:8], results[8].T, *results[9:])
+
+
+def place_kernel(
+    out_i,
+    gin_i,
+    gw,
+    ng,
+    out_o,
+    gin_o,
+    gq,
+    gk,
+    gv,
+    go,
+    gg,
+    gu,
+    gd,
+    n0,
+    n1,
+    n2,
+    n3,
+    OUT,
+    GIN,
+    GW,
+    NB,
+    sem,
+    osem,
+):
+    loads = [
+        pltpu.make_async_copy(src, dst, sem.at[i])
+        for i, (src, dst) in enumerate(
+            [
+                (gw.at[0], GW.at[0]),
+                (ng, NB),
+                (gw.at[1], GW.at[1]),
+                (gw.at[2], GW.at[2]),
+                (gw.at[3], GW.at[3]),
+                (out_i, OUT),
+                (gin_i, GIN),
+            ]
+        )
+    ]
+    for copy in loads:
+        copy.start()
+    stores = [
+        pltpu.make_async_copy(src, dst, osem.at[i])
+        for i, (src, dst) in enumerate(
+            [(GW.at[1], gg), (GW.at[2], gu), (GW.at[3], gd), (OUT, out_o), (GIN, gin_o)]
+        )
+    ]
+    for load, store in zip(loads[2:], stores):
+        load.wait()
+        store.start()
+    loads[0].wait()
+    two = 2 * HD
+    b = [GW[0, :, i * two : (i + 1) * two] for i in range(6)]
+    gq[...] = jnp.concatenate([b[0], b[3][:, :HD]], axis=1)
+    gk[...] = jnp.concatenate([b[1], b[3][:, HD:]], axis=1)
+    gv[...] = jnp.concatenate([b[2], b[4][:, :HD]], axis=1)
+    go[...] = jnp.concatenate([b[5], b[4][:, HD:]], axis=1).T
+    loads[1].wait()
+    for i, n in enumerate((n0, n1, n2, n3)):
+        n[...] = NB[i, :]
+    for store in stores:
+        store.wait()
 
 
 VMEM_BYTES = 64 << 20

time: 276 us -> 216 us (0.78)
  Pallas kernels: 253 us -> 213 us
  local copies, waits for them, and re-layouts: 16.8 us -> 0 us
  other arithmetic: 3.29 us -> 0 us
    pallas_call x1, Pallas kernels: 253 us -> 209 us  [layer_per_device(): pl.pallas_call(functools.partial(layer_kernel, nz), out_shape=(jax.ShapeD...]
    slice x11 -> x0, local copies, waits for them, and re-layouts: 6.06 us -> none  [the longest x1 1.52 us: layer_per_device(): norms[3]]
    reshape x4 -> x0, local copies, waits for them, and re-layouts: 5.07 us -> none  [layer_per_device(): v.reshape(1, width)]
    pallas_call x0 -> x1, Pallas kernels: none -> 3.51 us  [layer_per_device(): pl.pallas_call(place_kernel, out_shape=(jax.ShapeDtypeStruct(layer_input....]
    unnamed x8 -> x0, local copies, waits for them, and re-layouts: 3.39 us -> none
where the time goes in v2:
time: 216 us; the launch traced here: 214 us
  Pallas kernels  213 us (99%)
    pallas_call x1, Pallas kernels, layer_per_device(): pl.pallas_call(functools.partial(layer_kernel, nz), out_shape=(jax.ShapeD...  209 us

profile of v2, /device:TPU:0, one launch (start us, length us, event | category | flops | bytes accessed | tf_op | source)
XLA Modules:
  0.0 213.6 jit_solution(15666242864164269295)
XLA Ops:
  0.7 209.3 %shard_map.273 = (bf16[2,256,768]{2,1,0:T(8,128)(2,1)}, bf16[2,256,768]{2,1,0:T(8,128)(2,1)}, f32[4,96,768]{2,1,0:T(8,128)}, f32[8,768]{1,0:T(8,128)}) custom-call(bf16[2,256,768]{2,1,0:T(8,128)(2,1)} %xin.1, bf16[2,256,768]{2,1,0:T(8,128)(2,1)} %cot.1, s32[2,1024]{1,0:T(2,128)} %seg_h.1, bf16[96,192]{1,0:T(8,128)(2,1)} %wq_h.1, bf16[96,192]{1,0:T(8,128)(2,1)} %wk_h.1, ...), custom_call_target="tpu_custom_call" | custom-call | tf_op jit(solution)/shard_map/pallas_call | solution.py:1248
  210.0 3.5 %shard_map.274 = (bf16[2,256,768]{2,1,0:T(8,128)(2,1)}, bf16[2,256,768]{2,1,0:T(8,128)(2,1)}, f32[96,192]{1,0:T(8,128)}, f32[96,192]{1,0:T(8,128)}, f32[96,192]{...) custom-call(bf16[2,256,768]{2,1,0:T(8,128)(2,1)} %get-tuple-element., ...), custom_call_target="tpu_custom_call" | custom-call | tf_op jit(solution)/shard_map/pallas_call | solution.py:1286

commit v3 on v2

--- a/solution.py
+++ b/solution.py
@@ -519,9 +519,18 @@
     pl.semaphore_wait(barrier, len(peers))
 
     ag = {}
-    half_cols = width // 2
-    pieces = [(0, 0, width), (1, 0, width), (2, 0, width), (3, 0, half_cols), (3, half_cols, half_cols)]
-    LAST = 4
+    split = width // 3
+    pieces = [
+        (0, 0, width),
+        (1, 0, width),
+        (2, 0, width),
+        (3, 0, split),
+        (3, split, width - split),
+        (0, 0, 3 * LANES),
+        (0, 3 * LANES, 2 * LANES),
+        (0, 5 * LANES, LANES),
+    ]
+    LAST, QKV, REST, OUT = 4, 5, 6, 7
 
     def cut(view, p):
         _, lo, n = pieces[p]
@@ -590,10 +599,12 @@
         for copy in ag[p, "z"] + ag[p, "x"] + ag[p, "y"] + ag[p, "d"]:
             sent(copy)
 
+    e1(0)
+    e1(3)
+    e1_plane(LAST)
+    e1(2)
     x_far = rc(xin.at[1 - xi], X.at[tt], dev_x)
     x_core = rc(xin.at[xi], X.at[tt], dev_c)
-    e1(0)
-    e1_plane(LAST)
 
     l_seg.wait()
     seg = SEG
@@ -621,6 +632,9 @@
 
         lax.fori_loop(0, 4, step, 0)
 
+    f2(LAST)
+    e1(1)
+    e2(0)
     x_far.wait_recv()
     x_core2 = rc(X.at[t_x], X.at[t_x], dev_c)
     x_core.wait_recv()
@@ -630,9 +644,8 @@
         copy.wait()
     x_core2.wait_recv()
     turn_rows(X, XT)
-    e2(0)
-    e1(1)
-    f2(LAST)
+    e2(3)
+    f3(LAST)
     e3(0, 1)
 
     def project(s):
@@ -701,19 +714,17 @@
         lax.fori_loop(0, 4, turn, 0)
 
     project(0)
-    e2(1)
-    e1(2)
+    e2(2)
+    e3(3, 1)
     e4(0)
     project(1)
+    e2(1)
     attend(0, 2)
+    e3(2, 2)
+    attend(2, 2)
+    e4(3)
+    attend(4, 2)
     e3(1, 2)
-    e2(2)
-    e1(3)
-    attend(2, 2)
-    ct_far = rc(cot.at[1 - xi], CT.at[xi], dev_x)
-    f3(LAST)
-    attend(4, 2)
-    e4(1)
     turn_heads(0)
     turn_heads(1)
     last_exchange = []
@@ -745,6 +756,7 @@
         return mt(ATT[0, at, :], wmat(0, 0, 4 * LANES)) + mt(ATT[1, at, :], wmat(0, 1, 4 * LANES))
 
     exchange(0, out_part)
+    ct_far = rc(cot.at[1 - xi], CT.at[xi], dev_x)
     tile = quarter // 2
 
     def over_tiles(fn):
@@ -764,11 +776,9 @@
 
     over_tiles(first_norm)
     h_copies = spread()
-    e3(2, 1)
     for copy in h_copies:
         copy.wait_recv()
     turn_rows(F4, TT)
-    e2(3)
 
     def ff_up(s, i):
         at = at_quarter(i)
@@ -781,9 +791,8 @@
 
     lax.fori_loop(0, 4, lambda i, _: ff_up(0, i), 0)
     e4(2)
-    e3(3, 1)
+    e4(1)
     lax.fori_loop(0, 4, lambda i, _: ff_up(1, i), 0)
-    e4(3)
     f4(LAST)
 
     def down_part(i):
@@ -814,7 +823,7 @@
 
     slots = {3: G, 1: W.at[3], 2: W.at[1], 0: W.at[2]}
     rs = {}
-    by_x = {0: 1, 1: 1, 2: 1, 3: 2}
+    by_x = {1: 1, 2: 2, 3: 1, QKV: 2, REST: 2, OUT: 1}
 
     def g_at(p, s, zz, yy):
         return cut(slots[pieces[p][0]].at[s, zz, yy], p)
@@ -920,15 +929,25 @@
 
         lax.fori_loop(0, nz, step, 0)
 
+
+    def turn_half(first):
+        def step(k, _):
+            i = first + 2 * k
+            DT[:, at_quarter(i)] = F4[i].T
+            return 0
+
+        lax.fori_loop(0, 2, step, 0)
+
+    turn_half(c)
     for copy in d_copies:
         copy.wait_recv()
-    turn_rows(F4, DT)
+    turn_half(1 - c)
     weight_grad(LAST, 0, DT, RR)
     weight_grad(LAST, 1, DT, RR)
     q1(LAST)
     weight_grad(3, 1, DT, RR)
+    weight_grad(3, 0, DT, RR)
     r1_far(3)
-    weight_grad(3, 0, DT, RR)
     r1_near(3)
 
     def ff_back(n, _):
@@ -944,13 +963,12 @@
         return 0
 
     lax.fori_loop(0, 8, ff_back, 0)
-    r2(3)
     e_sent(3)
     e_sent(LAST)
     weight_grad(1, 1, TT, GP)
     r1_far(1)
     weight_grad(1, 0, TT, GP)
-    r1_near(1)
+    r2(3)
 
     def hidden_part(i):
         at = at_quarter(i)
@@ -979,19 +997,17 @@
     n_core = rc(NG, NR.at[0], dev_c)
     e_sent(1)
     e_sent(2)
+    r1_near(1)
     weight_grad(2, 1, TT, UP)
-    r1_far(2)
+    r2(1)
     weight_grad(2, 0, TT, UP)
-    r1_near(2)
-    r3(3)
-    r2(1)
     for copy in b_copies:
         copy.wait_recv()
     n_core.wait_recv()
     NS[0] = NG[...] + NR[0]
     n_x = rc(NS.at[0], NR.at[1], dev_x)
     turn_rows(F4, DT)
-
+    r1_far(2)
     def out_grad(n, _):
         s = lax.div(n, nz)
         j = lax.rem(n, nz)
@@ -1032,8 +1048,6 @@
     n_x.wait_recv()
     NS[1] = NS[0] + NR[1]
     n_y = rc(NS.at[1], NR.at[2], dev_y)
-    q2(LAST)
-
     def attend_back(s, first, heads):
         def head(hh, _):
             h = 3 * s + hh
@@ -1094,45 +1108,56 @@
 
         lax.fori_loop(0, 4, gather, 0)
 
-    def in_grad(s):
+    def in_grad(s, p):
         block = NY * rows
+        _, lo, n = pieces[p]
 
         def step(j, _):
             at = pl.ds(pl.multiple_of(j * block, block), block)
-            part = mm(XT[at, :], RR[s, :, : 5 * LANES])
-            mixed = slots[0][s, j, :, :, 4 * LANES : 5 * LANES].reshape(block, LANES)
-            mixed = (part[:, 4 * LANES :] + mixed.astype(F32)).astype(BF16)
-            slots[0][s, j, :, :, : 4 * LANES] = (
-                part[:, : 4 * LANES].astype(BF16).reshape(NY, rows, 4 * LANES)
-            )
-            slots[0][s, j, :, :, 4 * LANES : 5 * LANES] = mixed.reshape(NY, rows, LANES)
+            part = mm(XT[at, :], RR[s, :, lo : lo + n])
+            if p == REST:
+                mixed = slots[0][s, j, :, :, 4 * LANES : 5 * LANES].reshape(block, LANES)
+                mixed = (part[:, LANES:] + mixed.astype(F32)).astype(BF16)
+                part = part[:, :LANES]
+                slots[0][s, j, :, :, 4 * LANES : 5 * LANES] = mixed.reshape(NY, rows, LANES)
+                n_out = LANES
+            else:
+                n_out = n
+            slots[0][s, j, :, :, lo : lo + n_out] = part.astype(BF16).reshape(NY, rows, n_out)
             return 0
 
         lax.fori_loop(0, nz, step, 0)
 
     attend_back(1, 0, 1)
+    r1_near(2)
+    r3(3)
+    attend_back(1, 1, 1)
+    r3(1)
+    attend_back(1, 2, 1)
     r2(2)
-    r3(1)
-    attend_back(1, 1, 2)
-    q3(LAST)
-    r4(3)
     join_heads(1)
-    in_grad(1)
-    r1_far(0)
+    r1_far(OUT)
+    in_grad(1, QKV)
+    r1_far(QKV)
+    in_grad(1, REST)
+    r1_near(OUT)
     n_y.wait_recv()
     NS[2] = NS[1] + NR[2]
     NZR[z] = NS[2]
     n_z = [rc(NS.at[2], NZR.at[z], dev_z[j]) for j in range(1, nz)]
     attend_back(0, 0, 2)
+    r1_far(REST)
     r3(2)
-    q4(LAST)
     attend_back(0, 2, 1)
+    r2(OUT)
     join_heads(0)
-    in_grad(0)
-    r1_near(0)
-    r2(0)
-    r4(1)
-
+    in_grad(0, QKV)
+    r1_near(QKV)
+    r2(QKV)
+    q2(LAST)
+    r4(3)
+    in_grad(0, REST)
+    r1_near(REST)
     def input_part(i):
         at = at_quarter(i)
         return mt(RR[0, at, : 5 * LANES], wmat(0, 0, 0, 5 * LANES)) + mt(
@@ -1146,22 +1171,30 @@
         OB[1, k, at, :] = g.astype(BF16)
 
     over_tiles(input_grad)
+    r3(OUT)
+    r2(REST)
     i_far = rc(OB.at[1, 1 - xi], gin_h.at[xi], dev_x)
     i_own = lc(OB.at[1, xi], gin_h.at[xi])
-    r4(2)
+    r4(1)
+    r3(QKV)
+    q3(LAST)
     for copy in n_z:
         copy.wait_recv()
     total = NZR[0]
     for j in range(1, nz):
         total = total + NZR[j]
     ng_out[...] = total
-    r3(0)
-    r4(0)
+    r3(REST)
+    r4(OUT)
+    r4(2)
+    r4(QKV)
+    q4(LAST)
+    r4(REST)
     o_far.wait_recv()
     i_far.wait_recv()
     o_own.wait()
     i_own.wait()
-    for p in range(5):
+    for p in (1, 2, 3, LAST, QKV, REST, OUT):
         rs[p, "out"].wait()
     for copy in list(sends.values()):
         sent(copy)
@@ -1192,7 +1225,7 @@
     anywhere = pl.BlockSpec(memory_space=pl.ANY)
     vmem = pl.BlockSpec(memory_space=pltpu.VMEM)
     half = HD // 2
-    copies = 134
+    copies = 152
     part = query_weight.shape[1]
     scratch = [
         ((4, 2, nz, NY, rows, width), BF16),
@@ -1243,7 +1276,7 @@
         ((3, 8, width), F32),
         ((3, 8, width), F32),
         ((nz, 8, width), F32),
-        ((nz, 2, NY, rows, width // 2), BF16),
+        ((nz, 2, NY, rows, width - width // 3), BF16),
     ]
     outputs, grad_input, grads, norms = pl.pallas_call(
         functools.partial(layer_kernel, nz),
@@ -1257,7 +1290,7 @@
         out_specs=(anywhere, anywhere, anywhere, vmem),
         scratch_shapes=[pltpu.VMEM(shape, kind) for shape, kind in scratch]
         + [
-            pltpu.SemaphoreType.DMA((25,)),
+            pltpu.SemaphoreType.DMA((27,)),
             pltpu.SemaphoreType.DMA((copies,)),
             pltpu.SemaphoreType.DMA((copies,)),
         ],

time: 216 us -> 198 us (0.917); the launches traced: 214 us -> 198 us
  Pallas kernels: 213 us -> 197 us
    pallas_call x1, Pallas kernels: 209 us -> 194 us  [layer_per_device(): pl.pallas_call(functools.partial(layer_kernel, nz), out_shape=(jax.ShapeD...]
where the time goes in v3:
time: 198 us
  Pallas kernels  197 us (99%)
    pallas_call x1, Pallas kernels, layer_per_device(): pl.pallas_call(functools.partial(layer_kernel, nz), out_shape=(jax.ShapeD...  194 us

profile of v3, /device:TPU:0, one launch (start us, length us, event | category | flops | bytes accessed | tf_op | source)
XLA Modules:
  0.0 198.2 jit_solution(17862120323203137400)
XLA Ops:
  0.7 193.9 %shard_map.273 = (bf16[2,256,768]{2,1,0:T(8,128)(2,1)}, bf16[2,256,768]{2,1,0:T(8,128)(2,1)}, f32[4,96,768]{2,1,0:T(8,128)}, f32[8,768]{1,0:T(8,128)}) custom-call(bf16[2,256,768]{2,1,0:T(8,128)(2,1)} %xin.1, bf16[2,256,768]{2,1,0:T(8,128)(2,1)} %cot.1, s32[2,1024]{1,0:T(2,128)} %seg_h.1, bf16[96,192]{1,0:T(8,128)(2,1)} %wq_h.1, bf16[96,192]{1,0:T(8,128)(2,1)} %wk_h.1, ...), custom_call_target="tpu_custom_call" | custom-call | tf_op jit(solution)/shard_map/pallas_call | solution.py:1281
  194.5 3.5 %shard_map.274 = (bf16[2,256,768]{2,1,0:T(8,128)(2,1)}, bf16[2,256,768]{2,1,0:T(8,128)(2,1)}, f32[96,192]{1,0:T(8,128)}, f32[96,192]{1,0:T(8,128)}, f32[96,192]{...) custom-call(bf16[2,256,768]{2,1,0:T(8,128)(2,1)} %get-tuple-element., ...), custom_call_target="tpu_custom_call" | custom-call | tf_op jit(solution)/shard_map/pallas_call | solution.py:1319
